TPU v7x, 32 devices: a whole 2x2x4 slice. The times are simulated.
32 devices in a mesh: dp: 2 (over x), row: 4 (over z), col: 4 (over y, core).
Axes of the slice: x: 2, y: 2, z: 4, core: 2. Of those that a mesh axis runs over, the one named last changes fastest.
Arguments:
- features: bfloat16 [2, 128, 128, 320], P('dp', 'row', 'col'), may hold values from -20 to 20
- norm1_gain: float32 [320], replicated, may hold values from 0.1 to 1.9
- conv1_kernel: bfloat16 [320, 9, 320], P('dp'), may hold values from -0.109375 to 0.109375
- norm2_gain: float32 [320], replicated, may hold values from 0.1 to 1.9
- conv2_kernel: bfloat16 [320, 9, 320], P('dp'), may hold values from -0.109375 to 0.109375
Outputs:
- block_out: bfloat16 [2, 128, 128, 320], P('dp', 'row', 'col')
All inputs are finite; a program needn't handle non-finite values.
Results may differ from a plain program's by a relative error of at most 0.007.
Values may be sent and summed in bfloat16 or wider, within the bound.
No kernel may reach another device: no remote copies, remote signals or barrier semaphores. Data moves between devices by JAX's collectives and lax.ppermute only.
A program may use at most 64 MiB of HBM per device.

v0:
```python
import jax
import jax.numpy as jnp
from jax import lax
from jax.sharding import PartitionSpec as P

GROUPS = 32


EPS = 1e-05


def extended(value, sides, width):
    for axis, dim in sides:
        size, length = (lax.axis_size(axis), value.shape[dim])
        up = [(i, (i + 1) % size) for i in range(size - 1)]
        down = [(j, i) for i, j in up]
        last = lax.slice_in_dim(value, length - width, length, axis=dim)
        initial = lax.slice_in_dim(value, 0, width, axis=dim)
        before = lax.ppermute(last, axis, up)
        after = lax.ppermute(initial, axis, down)
        value = jnp.concatenate([before, value, after], axis=dim)
    return value


def normalize(values, scale_gain, count):
    batch_dev, tile_rows, tile_cols, width = values.shape
    grouped = values.astype(jnp.float32).reshape(
        batch_dev, tile_rows * tile_cols, GROUPS, width // GROUPS
    )
    totals, squares = lax.psum(
        (jnp.sum(grouped, axis=(1, 3)), jnp.sum(grouped * grouped, axis=(1, 3))), ("row", "col")
    )
    average_flat = totals / count
    spread = squares / count - average_flat * average_flat
    centred = grouped - average_flat[:, None, :, None]
    scaled = centred * lax.rsqrt(spread + EPS)[:, None, :, None]
    normed = scaled.reshape(values.shape) * scale_gain
    return jax.nn.silu(normed).astype(jnp.bfloat16)


def tap_stack(values):
    padded = extended(values, (("row", 1), ("col", 2)), 1)
    tile_rows, tile_cols, width = (values.shape[1], values.shape[2], values.shape[3])
    pieces = [
        padded[:, shift_row : shift_row + tile_rows, shift_col : shift_col + tile_cols, :]
        for shift_row in range(3)
        for shift_col in range(3)
    ]
    return jnp.concatenate(pieces, axis=-1).reshape(-1, 9 * width)


def finish(stacked, whole_kernel, skip_flat):
    flat_kernel = whole_kernel.reshape(whole_kernel.shape[0], -1)
    result = lax.dot_general(
        stacked, flat_kernel, (((1,), (1,)), ((), ())), preferred_element_type=jnp.float32
    )
    if skip_flat is not None:
        result = result + skip_flat.astype(jnp.float32)
    return result.astype(jnp.bfloat16)


def convolve_gathered(stacked, kernel, skip_flat):
    whole_kernel = lax.all_gather(kernel, "dp", axis=0, tiled=True)
    return finish(stacked, whole_kernel, skip_flat)


def local(features, norm1_gain, conv1_kernel, norm2_gain, conv2_kernel):
    batch_dev, tile_rows, tile_cols, width = features.shape
    count = tile_rows * tile_cols * lax.axis_size("row") * lax.axis_size("col") * (width // GROUPS)
    first_act = normalize(features, norm1_gain, count)
    first_stack = tap_stack(first_act)
    middle = convolve_gathered(first_stack, conv1_kernel, None)
    middle = middle.reshape(batch_dev, tile_rows, tile_cols, width)
    second_act = normalize(middle, norm2_gain, count)
    second_stack = tap_stack(second_act)
    skip_flat = features.reshape(-1, width)
    block_out = convolve_gathered(second_stack, conv2_kernel, skip_flat)
    return block_out.reshape(batch_dev, tile_rows, tile_cols, width)


def solution(mesh):
    return jax.shard_map(
        local,
        mesh=mesh,
        in_specs=(P("dp", "row", "col", None), P(), P("dp", None, None), P(), P("dp", None, None)),
        out_specs=P("dp", "row", "col", None),
        check_vma=False,
    )
```

profile of v0, /device:TPU:0, one launch (start us, length us, event | category | flops | bytes accessed | tf_op | source)
XLA Modules:
  0.0 162.0 jit_solution(10472760439591955007)
XLA Ops:
  7.3 1.4 convert_reduce_fusion
  9.2 35.0 %all-reduce.1 = (f32[1,32]{1,0:T(1,128)S(1)}, f32[1,32]{1,0:T(1,128)S(1)}) all-reduce(f32[1,32]{1,0:T(1,128)S(1)} %bitcast.63, f32[1,32]{1,0:T(1,128)S(1)} %bitcast.61), channel_id=1, replica_groups=mesh['dp'=2,'row'=4,'col'=4] {'row','col'}, use_global_device_ids=true, to_apply=%region_5.6 | all-reduce | flops 64 | bytes 512 | tf_op jit(solution)/shard_map/psum | solution.py:30
  44.5 1.2 multiply_convert_fusion.1
  45.7 1.3 collective-permute-start
  47.0 1.3 collective-permute-start.1
  48.5 4.2 %collective-permute-done.1 = bf16[1,1,32,320]{3,2,1,0:T(8,128)(2,1)S(1)} collective-permute-done((bf16[1,1,32,320]{3,2,1,0:T(8,128)(2,1)S(1)}, bf16[1,1,32,320]{3,2,1,0:T(8,128)(2,1)S(1)}, u32[]{:S(2)}, u32[]{:S(2)}) %collective-permute-start.1) | collective-permute-done | bytes 20512 | tf_op jit(solution)/shard_map/ppermute | solution.py:20
  52.8 1.3 collective-permute-start.2
  54.1 1.3 collective-permute-start.3
  55.4 1.4 pad_maximum_fusion.4
  57.9 1.9 %fusion.6 = (bf16[1,32,32,320]{3,2,1,0:T(8,128)(2,1)S(1)}, bf16[1,32,32,320]{3,2,1,0:T(8,128)(2,1)S(1)}, bf16[1,32,32,320]{3,2,1,0:T(8,128)(2,1)}, bf16[1,32,32,...) fusion(bf16[1,34,33,320]{3,2,1,0:T(8,128)(2,1)S(1)} %get-tuple-element.29, ...), kind=kLoop, calls=%fused_computation.40 | loop fusion | bytes 7864320 | tf_op jit(solution)/shard_map/slice | solution.py:45
  59.8 10.1 %concatenate.96 = bf16[1024,2880]{1,0:T(8,128)(2,1)} concatenate(bf16[1024,320]{1,0:T(8,128)(2,1)} %bitcast.45, bf16[1024,320]{1,0:T(8,128)(2,1)} %bitcast.50, bf16[1024,320]{1,0:T(8,128)(2,1)} %bitcast.44, bf16[1024,320]{1,0:T(8,128)(2,1)} %bitcast.46, bf16[1024,320]{1,0:T(8,128)(2,1)S(1)} %bitcast.39, bf16[1024,320]{1,0:T(8,128)(2,1)S(1)} %bitcast.43, ...), dimensions={1} | concatenate | bytes 11796480 | tf_op jit(solution)/shard_map/concatenate | solution.py:49
  69.9 4.2 %copy.17 = bf16[320,9,320]{0,2,1:T(8,128)(2,1)} copy(bf16[320,9,320]{2,0,1:T(8,128)(2,1)} %all-gather.3.cloned.1.call-done) | data formatting | bytes 3686400 | tf_op jit(solution)/shard_map/all_gather | solution.py:63
  74.1 6.7 %fusion.3 = (f32[320]{0:T(512)S(1)}, f32[320]{0:T(512)S(1)}, f32[1024,320]{0,1:T(8,128)}) fusion(bf16[1024,2880]{1,0:T(8,128)(2,1)} %concatenate.96, bf16[320,2880]{0,1:T(8,128)(2,1)} %bitcast.59), kind=kOutput, calls=%fused_computation.37 | convolution fusion | flops 1889074688 | bytes 9054720 | tf_op jit(solution)/shard_map/dot_general | solution.py:54
  81.3 30.2 %all-reduce = (f32[1,32]{1,0:T(1,128)S(1)}, f32[1,32]{1,0:T(1,128)S(1)}) all-reduce(f32[1,32]{1,0:T(1,128)S(1)} %bitcast.62, f32[1,32]{1,0:T(1,128)S(1)} %bitcast.60), channel_id=1, replica_groups=mesh['dp'=2,'row'=4,'col'=4] {'row','col'}, use_global_device_ids=true, to_apply=%region_11.12 | all-reduce | flops 64 | bytes 512 | tf_op jit(solution)/shard_map/psum | solution.py:30
  111.8 1.8 %copy.18 = f32[1024,320]{1,0:T(8,128)S(1)} copy(f32[1024,320]{0,1:T(8,128)} %get-tuple-element.45) | data formatting | bytes 2621440 | tf_op jit(solution)/shard_map/convert_element_type | solution.py:27
  114.1 1.3 collective-permute-start.4
  115.4 1.3 collective-permute-start.5
  116.7 1.4 copy.28
  118.1 4.2 %copy.27 = bf16[320,9,320]{0,2,1:T(8,128)(2,1)} copy(bf16[320,9,320]{2,0,1:T(8,128)(2,1)} %all-gather.5.cloned.1.call-done) | data formatting | bytes 3686400 | tf_op jit(solution)/shard_map/all_gather | solution.py:63
  122.4 1.3 collective-permute-start.6
  123.7 1.5 collective-permute-start.7
  126.5 1.1 copy.25
  129.6 2.0 %constant_dynamic-update-slice_fusion.7 = bf16[1024,2880]{0,1:T(8,128)(2,1)} fusion(bf16[1024,320]{0,1:T(8,128)(2,1)} %copy.19), kind=kLoop, calls=%fused_computation.32 | loop fusion | bytes 1310720
  131.6 1.5 fusion.4
  133.1 1.1 copy.21
  136.3 2.0 %constant_dynamic-update-slice_fusion.5 = bf16[1024,2880]{0,1:T(8,128)(2,1)} fusion(bf16[1024,2880]{0,1:T(8,128)(2,1)} %constant_dynamic-update-slice_fusion.6, bf16[1024,320]{0,1:T(8,128)(2,1)} %copy.21), kind=kLoop, calls=%fused_computation.30 | loop fusion | bytes 1310720
  139.2 1.4 fusion.2
  140.6 2.2 %copy.23 = bf16[1024,320]{0,1:T(8,128)(2,1)} copy(bf16[1024,320]{1,0:T(8,128)(2,1)} %bitcast.52) | data formatting | bytes 1310720 | tf_op jit(solution)/shard_map/concatenate | solution.py:49
  142.8 1.2 copy.24
  144.3 2.1 %constant_dynamic-update-slice_fusion.3 = bf16[1024,2880]{0,1:T(8,128)(2,1)} fusion(bf16[1024,2880]{0,1:T(8,128)(2,1)} %fusion.2, bf16[1024,320]{0,1:T(8,128)(2,1)} %copy.23), kind=kLoop, calls=%fused_computation.28 | loop fusion | bytes 1310720
  149.1 4.9 %fusion = bf16[1024,320]{0,1:T(8,128)(2,1)S(1)} fusion(f32[1024,320]{0,1:T(8,128)S(1)} %copy-done.8, bf16[1024,2880]{0,1:T(8,128)(2,1)} %constant_dynamic-update-slice_fusion, bf16[320,2880]{0,1:T(8,128)(2,1)S(1)} %bitcast.58), kind=kOutput, calls=%fused_computation.4 | convolution fusion | flops 1888092160 | bytes 9707520 | tf_op jit(solution)/shard_map/dot_general | solution.py:54
  154.0 1.2 copy.29
  (69 shorter events, 13.5 us)
Async XLA Ops:
  6.5 38.0 %copy-start = (bf16[1,32,32,320]{3,2,1,0:T(8,128)(2,1)S(1)}, bf16[1,32,32,320]{3,2,1,0:T(8,128)(2,1)}, u32[]{:S(2)}) copy-start(bf16[1,32,32,320]{3,2,1,0:T(8,128)(2,1)} %param.5) | copy-start | bytes 1966084
  6.5 63.4 %all-gather.3.cloned.1.call-start = ((), (), s32[]{:S(2)}) async-start(), calls=%async_computation | async-start | bytes 3317760 | tf_op jit(solution)/shard_map/all_gather | solution.py:63
  7.3 110.8 %all-gather.5.cloned.1.call-start = ((), (), s32[]{:S(2)}) async-start(), calls=%async_computation.1 | async-start | bytes 3317760 | tf_op jit(solution)/shard_map/all_gather | solution.py:63
  45.7 2.8 %collective-permute-start = (bf16[1,1,32,320]{3,2,1,0:T(8,128)(2,1)S(1)}, bf16[1,1,32,320]{3,2,1,0:T(8,128)(2,1)S(1)}, u32[]{:S(2)}, u32[]{:S(2)}) collective-permute-start(bf16[1,1,32,320]{3,2,1,0:T(8,128)(2,1)S(1)} %get-tuple-element.39), channel_id=1, source_target_pairs={{0,4},{4,8},{8,12},{1,5},{5,9},{9,13},{2,6},{6,10},{10,14},{3,7},{... | collective-permute-start | bytes 61448 | tf_op jit(solution)/shard_map/ppermute | solution.py:19
  47.0 5.7 %collective-permute-start.1 = (bf16[1,1,32,320]{3,2,1,0:T(8,128)(2,1)S(1)}, bf16[1,1,32,320]{3,2,1,0:T(8,128)(2,1)S(1)}, u32[]{:S(2)}, u32[]{:S(2)}) collective-permute-start(bf16[1,1,32,320]{3,2,1,0:T(8,128)(2,1)S(1)} %get-tuple-element.40), channel_id=1, source_target_pairs={{4,0},{8,4},{12,8},{5,1},{9,5},{13,9},{6,2},{10,6},{14,10},{7,3},{... | collective-permute-start | bytes 61448 | tf_op jit(solution)/shard_map/ppermute | solution.py:20
  52.8 4.0 %collective-permute-start.2 = (bf16[1,34,1,320]{3,2,1,0:T(2,128)(2,1)S(1)}, bf16[1,34,1,320]{3,2,1,0:T(2,128)(2,1)S(1)}, u32[]{:S(2)}, u32[]{:S(2)}) collective-permute-start(bf16[1,34,1,320]{3,2,1,0:T(2,128)(2,1)S(1)} %get-tuple-element.32), channel_id=1, source_target_pairs={{0,1},{1,2},{2,3},{4,5},{5,6},{6,7},{8,9},{9,10},{10,11},{12,13},{... | collective-permute-start | bytes 65288 | tf_op jit(solution)/shard_map/ppermute | solution.py:19
  54.1 3.1 %collective-permute-start.3 = (bf16[1,34,1,320]{3,2,1,0:T(2,128)(2,1)S(1)}, bf16[1,34,1,320]{3,2,1,0:T(2,128)(2,1)S(1)}, u32[]{:S(2)}, u32[]{:S(2)}) collective-permute-start(bf16[1,34,1,320]{3,2,1,0:T(2,128)(2,1)S(1)} %get-tuple-element.31), channel_id=1, source_target_pairs={{1,0},{2,1},{3,2},{5,4},{6,5},{7,6},{9,8},{10,9},{11,10},{13,12},{... | collective-permute-start | bytes 65288 | tf_op jit(solution)/shard_map/ppermute | solution.py:20
  80.8 32.8 %copy-start.9 = (f32[320]{0:T(512)S(1)}, f32[320]{0:T(512)}, u32[]{:S(2)}) copy-start(f32[320]{0:T(512)} %param.8) | copy-start | bytes 3844
  114.1 8.2 %collective-permute-start.4 = (bf16[1,1,32,320]{3,2,1,0:T(8,128)(2,1)S(1)}, bf16[1,1,32,320]{3,2,1,0:T(8,128)(2,1)S(1)}, u32[]{:S(2)}, u32[]{:S(2)}) collective-permute-start(bf16[1,1,32,320]{3,2,1,0:T(8,128)(2,1)S(1)} %get-tuple-element.35), channel_id=1, source_target_pairs={{0,4},{4,8},{8,12},{1,5},{5,9},{9,13},{2,6},{6,10},{10,14},{3,7},{... | collective-permute-start | bytes 61448 | tf_op jit(solution)/shard_map/ppermute | solution.py:19
  115.4 6.9 %collective-permute-start.5 = (bf16[1,1,32,320]{3,2,1,0:T(8,128)(2,1)S(1)}, bf16[1,1,32,320]{3,2,1,0:T(8,128)(2,1)S(1)}, u32[]{:S(2)}, u32[]{:S(2)}) collective-permute-start(bf16[1,1,32,320]{3,2,1,0:T(8,128)(2,1)S(1)} %get-tuple-element.36), channel_id=1, source_target_pairs={{4,0},{8,4},{12,8},{5,1},{9,5},{13,9},{6,2},{10,6},{14,10},{7,3},{... | collective-permute-start | bytes 61448 | tf_op jit(solution)/shard_map/ppermute | solution.py:20
  122.4 5.3 %collective-permute-start.6 = (bf16[1,34,1,320]{3,2,1,0:T(2,128)(2,1)S(1)}, bf16[1,34,1,320]{3,2,1,0:T(2,128)(2,1)S(1)}, u32[]{:S(2)}, u32[]{:S(2)}) collective-permute-start(bf16[1,34,1,320]{3,2,1,0:T(2,128)(2,1)S(1)} %get-tuple-element.28), channel_id=1, source_target_pairs={{0,1},{1,2},{2,3},{4,5},{5,6},{6,7},{8,9},{9,10},{10,11},{12,13},{... | collective-permute-start | bytes 65288 | tf_op jit(solution)/shard_map/ppermute | solution.py:19
  123.7 4.0 %collective-permute-start.7 = (bf16[1,34,1,320]{3,2,1,0:T(2,128)(2,1)S(1)}, bf16[1,34,1,320]{3,2,1,0:T(2,128)(2,1)S(1)}, u32[]{:S(2)}, u32[]{:S(2)}) collective-permute-start(bf16[1,34,1,320]{3,2,1,0:T(2,128)(2,1)S(1)} %get-tuple-element.27), channel_id=1, source_target_pairs={{1,0},{2,1},{3,2},{5,4},{6,5},{7,6},{9,8},{10,9},{11,10},{13,12},{... | collective-permute-start | bytes 65288 | tf_op jit(solution)/shard_map/ppermute | solution.py:20
  133.1 2.3 %copy-start.4 = (bf16[1024,320]{0,1:T(8,128)(2,1)S(1)}, bf16[1024,320]{0,1:T(8,128)(2,1)}, u32[]{:S(2)}) copy-start(bf16[1024,320]{0,1:T(8,128)(2,1)} %copy.20) | copy-start | bytes 1966084
  135.4 2.9 %copy-start.5 = (bf16[1024,320]{0,1:T(8,128)(2,1)S(1)}, bf16[1024,320]{0,1:T(8,128)(2,1)}, u32[]{:S(2)}) copy-start(bf16[1024,320]{0,1:T(8,128)(2,1)} %copy.22) | copy-start | bytes 1966084
  135.4 3.8 %copy-start.1 = (f32[1024,320]{0,1:T(8,128)S(1)}, f32[1024,320]{0,1:T(8,128)}, u32[]{:S(2)}) copy-start(f32[1024,320]{0,1:T(8,128)} %get-tuple-element.45) | copy-start | bytes 3932164
  139.2 4.8 %copy-start.2 = (bf16[1,32,32,320]{3,2,1,0:T(8,128)(2,1)S(1)}, bf16[1,32,32,320]{3,2,1,0:T(8,128)(2,1)}, u32[]{:S(2)}) copy-start(bf16[1,32,32,320]{3,2,1,0:T(8,128)(2,1)} %get-tuple-element.13) | copy-start | bytes 1966084
  144.0 2.4 %copy-start.6 = (bf16[1024,320]{0,1:T(8,128)(2,1)S(1)}, bf16[1024,320]{0,1:T(8,128)(2,1)}, u32[]{:S(2)}) copy-start(bf16[1024,320]{0,1:T(8,128)(2,1)} %copy.24) | copy-start | bytes 1966084
  144.0 3.3 %copy-start.3 = (bf16[1024,320]{0,1:T(8,128)(2,1)S(1)}, bf16[1024,320]{0,1:T(8,128)(2,1)}, u32[]{:S(2)}) copy-start(bf16[1024,320]{0,1:T(8,128)(2,1)} %copy.25) | copy-start | bytes 1966084
  146.4 2.7 %copy-start.7 = (bf16[320,9,320]{0,2,1:T(8,128)(2,1)S(1)}, bf16[320,9,320]{0,2,1:T(8,128)(2,1)}, u32[]{:S(2)}) copy-start(bf16[320,9,320]{0,2,1:T(8,128)(2,1)} %copy.27) | copy-start | bytes 5529604
  146.4 2.7 %copy-start.8 = (f32[1024,320]{0,1:T(8,128)S(1)}, f32[1024,320]{0,1:T(8,128)}, u32[]{:S(2)}) copy-start(f32[1024,320]{0,1:T(8,128)} %copy.28) | copy-start | bytes 3932164
Sparse Core Ops, SparseCore 0:
  8.9 37.0 all-gather.2
  48.5 33.7 all-gather.4
where the time goes:
time: 164 us; the launch traced here: 162 us
  blocking collectives  65.1 us (40%)
  local copies, waits for them, and re-layouts  47.5 us (29%)
  between operations  13.6 us (8%)
  matrix products  11.6 us (7%)
  starting transfers between devices  10.6 us (6%)
  other arithmetic  8 us (5%)
  waiting for transfers between devices  5.57 us (3%)
    psum x2, blocking collectives, normalize(): lax.psum((jnp.sum(grouped, axis=(1, 3)), jnp.sum(grouped * grouped, axis=...  65.1 us
    concatenate x10, local copies, waits for them, and re-layouts, tap_stack(): return jnp.concatenate(pieces, axis=-1).reshape(-1, 9 * width)  20.4 us
    dot_general x2, matrix products, finish(): lax.dot_general(stacked, flat_kernel, (((1,), (1,)), ((), ())), preferred...  11.6 us
    unnamed x27, local copies, waits for them, and re-layouts  9.62 us
    all_gather x2, local copies, waits for them, and re-layouts, convolve_gathered(): whole_kernel = lax.all_gather(kernel, 'dp', axis=0, tiled=True)  8.4 us
    ppermute x4, starting transfers between devices, extended(): after = lax.ppermute(initial, axis, down)  5.35 us
    ppermute x4, starting transfers between devices, extended(): before = lax.ppermute(last, axis, up)  5.17 us
    ppermute x4, waiting for transfers between devices, extended(): after = lax.ppermute(initial, axis, down)  4.66 us
  transfers between devices with their start and end apart: 10, of which 3 were waited for; matrix products, arithmetic and copies ran while one was open for 24% of the time, Pallas kernels for 0%

commit v1 on v0

v1 whole, which is shorter than its diff:
```python
import functools

import jax
import jax.numpy as jnp
from jax import lax
from jax.experimental import pallas as pl
from jax.experimental.pallas import tpu as pltpu
from jax.sharding import PartitionSpec as P

GROUPS = 32
EPS = 1e-05
ROWS = 16
F32 = jnp.float32
BF16 = jnp.bfloat16
MIB = 1 << 20


def split_rows(total, square):
    width = total.shape[1]
    at = lax.broadcasted_iota(jnp.int32, (ROWS, width), 0)
    out = jnp.zeros((ROWS, width), F32)
    for base, value in ((0, total), (3, square)):
        for step in range(3):
            part = value.astype(BF16).astype(F32)
            out = jnp.where(at == base + step, part, out)
            value = value - part
    return out.astype(BF16)


def join_rows(rows):
    return rows[0:1] + rows[1:2] + rows[2:3], rows[3:4] + rows[4:5] + rows[5:6]


def padded_lanes(width):
    return -(-3 * width // 128) * 128


def put_taps(store, taps, width):
    main = width // 128 * 128
    tail = width - main
    for e, tap in enumerate(taps):
        if main:
            store(e * main, main, tap[..., :main])
    if tail:
        for e, tap in enumerate(taps):
            store(3 * main + e * tail, tail, tap[..., main:])


def pack_body(kernel_ref, own_ref, send_ref, *, axis, parts):
    _, outs, width = kernel_ref.shape
    lanes = own_ref.shape[2]
    if 3 * width < lanes:
        own_ref[:, :, 3 * width :] = jnp.zeros((3, outs, lanes - 3 * width), BF16)
    for a in range(3):
        def store(at, size, value, a=a):
            own_ref[a, :, at : at + size] = value
        put_taps(store, [kernel_ref[3 * a + e] for e in range(3)], width)
    piece = outs // parts
    at = pl.multiple_of(lax.rem(lax.axis_index(axis), parts) * piece, ROWS)
    send_ref[...] = own_ref[:, pl.ds(at, piece), :]


def pack(kernel, axis, parts):
    outs, _, width = kernel.shape
    lanes = padded_lanes(width)
    return pl.pallas_call(
        functools.partial(pack_body, axis=axis, parts=parts),
        out_shape=(
            jax.ShapeDtypeStruct((3, outs, lanes), BF16),
            jax.ShapeDtypeStruct((3, outs // parts, lanes), BF16),
        ),
        compiler_params=pltpu.CompilerParams(vmem_limit_bytes=8 * MIB),
        name="pack",
    )(jnp.transpose(kernel, (1, 0, 2)))


def tile_stats(rows):
    return jnp.sum(rows, axis=0, keepdims=True), jnp.sum(rows * rows, axis=0, keepdims=True)


def put_messages(out_ref, rows, stats, up_ref, down_ref, own_ref):
    length, cells, width = out_ref.shape
    up_ref[:cells] = out_ref[length - 1]
    up_ref[cells:] = stats
    down_ref[:cells] = out_ref[0]
    down_ref[cells:] = stats
    own_ref[...] = stats


def first_body(tile_ref, up_ref, down_ref, own_ref):
    length, cells, width = tile_ref.shape
    total = jnp.zeros((1, width), F32)
    square = jnp.zeros((1, width), F32)
    step = 4
    for at in range(0, length, step):
        rows = tile_ref[at : at + step].reshape(step * cells, width).astype(F32)
        one, two = tile_stats(rows)
        total, square = total + one, square + two
    put_messages(tile_ref, None, split_rows(total, square), up_ref, down_ref, own_ref)


def message_shapes(cells, width):
    return (
        jax.ShapeDtypeStruct((cells + ROWS, width), BF16),
        jax.ShapeDtypeStruct((cells + ROWS, width), BF16),
        jax.ShapeDtypeStruct((ROWS, width), BF16),
    )


def first_messages(tile):
    length, cells, width = tile.shape
    return pl.pallas_call(
        first_body,
        out_shape=message_shapes(cells, width),
        compiler_params=pltpu.CompilerParams(vmem_limit_bytes=8 * MIB),
        name="first",
    )(tile)


def shifted(value, axis, by):
    size = lax.axis_size(axis)
    return lax.ppermute(value, axis, [(i, (i + by) % size) for i in range(size)])


def exchange(up, down, own, axis):
    size = lax.axis_size(axis)
    before = shifted(up, axis, 1)
    after = shifted(down, axis, size - 1)
    others = [shifted(own, axis, by) for by in range(2, size - 1)]
    return before, after, others


def summed(own_ref, before_ref, after_ref, other_refs, size):
    rows = own_ref[...].astype(F32)
    if size > 1:
        rows = rows + before_ref[before_ref.shape[0] - ROWS :].astype(F32)
    if size > 2:
        rows = rows + after_ref[after_ref.shape[0] - ROWS :].astype(F32)
    for other in other_refs:
        rows = rows + other[...].astype(F32)
    return join_rows(rows)


def edge_body(*refs, size, others):
    left_ref, right_ref, own_ref, before_ref, after_ref = refs[:5]
    other_refs = refs[5 : 5 + others]
    up_ref, down_ref, sum_ref = refs[5 + others :]
    length, width = left_ref.shape
    cells = before_ref.shape[0] - ROWS
    total, square = summed(own_ref, before_ref, after_ref, other_refs, size)
    stats = split_rows(total, square)
    sum_ref[...] = stats
    rows = up_ref.shape[0] - ROWS
    above = before_ref[:cells].astype(F32)
    below = after_ref[:cells].astype(F32)
    filler = jnp.zeros((rows - length - 2, width), F32)
    for out_ref, edge_ref, corner in ((up_ref, right_ref, cells - 1), (down_ref, left_ref, 0)):
        whole = [above[corner : corner + 1], edge_ref[...].astype(F32), below[corner : corner + 1], filler]
        out_ref[:rows] = jnp.concatenate(whole, axis=0).astype(BF16)
        out_ref[rows:] = stats


def edge_messages(left, right, own, before, after, others, size):
    length, width = left.shape
    rows = -(-(length + 2) // ROWS) * ROWS
    return pl.pallas_call(
        functools.partial(edge_body, size=size, others=len(others)),
        out_shape=message_shapes(rows, width),
        compiler_params=pltpu.CompilerParams(vmem_limit_bytes=8 * MIB),
        name="edge",
    )(left, right, own, before, after, *others)


def conv_body(*refs, pieces, others, size, count, skip, spread_axes, place):
    tile_ref, above_ref, below_ref, gain_ref, ones_ref, own_ref, left_ref, right_ref = refs[:8]
    at = 8
    other_refs = refs[at : at + others]
    at += others
    piece_refs = refs[at : at + pieces]
    at += pieces
    if skip:
        skip_ref = refs[at]
        at += 1
        out_ref = refs[at]
        at += 1
    else:
        out_ref, up_ref, down_ref, sum_ref = refs[at : at + 4]
        at += 4
    taps_ref, weight_ref, edge_ref, sems = refs[at:]

    length, cells, width = tile_ref.shape
    lanes = taps_ref.shape[2]
    copies = []
    for i, (piece, start) in enumerate(zip(piece_refs, place())):
        copy = pltpu.make_async_copy(
            piece, weight_ref.at[:, pl.ds(start, piece.shape[1]), :], sems.at[i]
        )
        copy.start()
        copies.append(copy)

    total, square = summed(own_ref, left_ref, right_ref, other_refs, size)
    grouped = jnp.dot(split_rows(total, square), ones_ref[...], preferred_element_type=F32)
    total, square = join_rows(grouped)
    average = total / count
    spread = jnp.maximum(square / count - average * average, 0.0)
    scale = lax.rsqrt(spread + EPS) * gain_ref[...]

    def act(value):
        normed = (value.astype(F32) - average) * scale
        return normed * (0.5 + 0.5 * jnp.tanh(0.5 * normed))

    row_axis, col_axis = spread_axes
    row, col = lax.axis_index(row_axis), lax.axis_index(col_axis)
    last_row, last_col = lax.axis_size(row_axis) - 1, lax.axis_size(col_axis) - 1
    rows = left_ref.shape[0] - ROWS
    edge_ref[0] = jnp.where(col > 0, act(left_ref[:rows]), 0.0)
    edge_ref[1] = jnp.where(col < last_col, act(right_ref[:rows]), 0.0)
    if 3 * width < lanes:
        taps_ref[:, :, 3 * width :] = jnp.zeros((length + 2, cells, lanes - 3 * width), BF16)
    where = lax.broadcasted_iota(jnp.int32, (cells, width), 0)

    def put_row(i, centre):
        left = jnp.where(where == 0, edge_ref[0, pl.ds(i, 1), :], pltpu.roll(centre, 1, 0))
        right = jnp.where(where == cells - 1, edge_ref[1, pl.ds(i, 1), :], pltpu.roll(centre, cells - 1, 0))

        def store(at, size, value):
            taps_ref[i, :, at : at + size] = value

        put_taps(store, [left.astype(BF16), centre.astype(BF16), right.astype(BF16)], width)

    def one_row(i, carry):
        put_row(i + 1, act(tile_ref[i]))
        return carry

    lax.fori_loop(0, length, one_row, 0, unroll=4)

    def border(i, source, inside):
        put_row(i, jnp.where(inside, act(source[:cells]), 0.0))
        for e in range(2):
            pass

    edge_ref[0, 0:1, :] = jnp.where(row > 0, edge_ref[0, 0:1, :], 0.0)
    edge_ref[1, 0:1, :] = jnp.where(row > 0, edge_ref[1, 0:1, :], 0.0)
    edge_ref[0, length + 1 : length + 2, :] = jnp.where(row < last_row, edge_ref[0, length + 1 : length + 2, :], 0.0)
    edge_ref[1, length + 1 : length + 2, :] = jnp.where(row < last_row, edge_ref[1, length + 1 : length + 2, :], 0.0)
    border(0, above_ref, row > 0)
    border(length + 1, below_ref, row < last_row)

    for copy in copies:
        copy.wait()

    outs = out_ref.shape[2]
    step = 8
    total = jnp.zeros((1, outs), F32)
    square = jnp.zeros((1, outs), F32)
    for start in range(0, length, step):
        result = None
        for a in range(3):
            part = lax.dot_general(
                taps_ref[start + a : start + a + step].reshape(step * cells, lanes),
                weight_ref[a],
                (((1,), (1,)), ((), ())),
                preferred_element_type=F32,
            )
            result = part if result is None else result + part
        if skip:
            result = result + skip_ref[start : start + step].reshape(step * cells, outs).astype(F32)
            out_ref[start : start + step] = result.astype(BF16).reshape(step, cells, outs)
        else:
            rounded = result.astype(BF16)
            out_ref[start : start + step] = rounded.reshape(step, cells, outs)
            one, two = tile_stats(rounded.astype(F32))
            total, square = total + one, square + two
    if not skip:
        put_messages(out_ref, None, split_rows(total, square), up_ref, down_ref, sum_ref)


def convolve(tile, above, below, gain, ones, own, left, right, others, pieces, place, count, skip):
    length, cells, width = tile.shape
    outs = width
    lanes = padded_lanes(width)
    rows = left.shape[0] - ROWS
    out = (jax.ShapeDtypeStruct((length, cells, outs), BF16),)
    if skip is None:
        out = out + message_shapes(cells, outs)
    vmem = pl.BlockSpec(memory_space=pltpu.VMEM)
    anywhere = pl.BlockSpec(memory_space=pl.ANY)
    skips = [] if skip is None else [skip]
    return pl.pallas_call(
        functools.partial(
            conv_body,
            pieces=len(pieces),
            others=len(others),
            size=lax.axis_size("col"),
            count=count,
            skip=skip is not None,
            spread_axes=("row", "col"),
            place=place,
        ),
        in_specs=[vmem] * (8 + len(others)) + [anywhere] * len(pieces) + [vmem] * len(skips),
        out_specs=(vmem,) * len(out),
        out_shape=out,
        scratch_shapes=[
            pltpu.VMEM((length + 2, cells, lanes), BF16),
            pltpu.VMEM((3, outs, lanes), BF16),
            pltpu.VMEM((2, rows, width), F32),
            pltpu.SemaphoreType.DMA((len(pieces),)),
        ],
        compiler_params=pltpu.CompilerParams(vmem_limit_bytes=24 * MIB),
        name="conv_skip" if skips else "conv",
    )(tile, above, below, gain, ones, own, left, right, *others, *pieces, *skips)


def gathered(kernel):
    outs = kernel.shape[0]
    size, cols = lax.axis_size("dp"), lax.axis_size("col")
    if size == 2 and cols % 2 == 0 and outs % (2 * ROWS) == 0:
        own, send = pack(kernel, "col", 2)
        got = lax.ppermute(send, "dp", [(0, 1), (1, 0)])
        mate = lax.ppermute(got, "col", [(i, i ^ 1) for i in range(cols)])
        piece = outs // 2

        def place():
            dp, half = lax.axis_index("dp"), lax.rem(lax.axis_index("col"), 2)
            other = (1 - dp) * outs
            return [
                pl.multiple_of(dp * outs, ROWS),
                pl.multiple_of(other + half * piece, ROWS),
                pl.multiple_of(other + (1 - half) * piece, ROWS),
            ]

        return [own, got, mate], place
    whole = lax.all_gather(kernel, "dp", axis=0, tiled=True)
    return [pack(whole, "col", 1)[0]], lambda: [0]


def normed_conv(tile, up, down, own, gain, ones, pieces, place, count, skip):
    above, below, others = exchange(up, down, own, "row")
    size = lax.axis_size("row")
    up, down, own = edge_messages(tile[:, 0], tile[:, -1], own, above, below, others, size)
    left, right, others = exchange(up, down, own, "col")
    return convolve(tile, above, below, gain, ones, own, left, right, others, pieces, place, count, skip)


def local(features, norm1_gain, conv1_kernel, norm2_gain, conv2_kernel):
    _, length, cells, width = features.shape
    members = width // GROUPS
    count = length * cells * lax.axis_size("row") * lax.axis_size("col") * members
    tile = features[0]
    group = jnp.arange(width) // members
    ones = (group[:, None] == group[None, :]).astype(BF16)
    pieces1, place1 = gathered(conv1_kernel)
    pieces2, place2 = gathered(conv2_kernel)
    up, down, own = first_messages(tile)
    middle, up, down, own = normed_conv(
        tile, up, down, own, norm1_gain[None], ones, pieces1, place1, count, None
    )
    (result,) = normed_conv(
        middle, up, down, own, norm2_gain[None], ones, pieces2, place2, count, tile
    )
    return result[None]


def solution(mesh):
    return jax.shard_map(
        local,
        mesh=mesh,
        in_specs=(P("dp", "row", "col", None), P(), P("dp", None, None), P(), P("dp", None, None)),
        out_specs=P("dp", "row", "col", None),
        check_vma=False,
    )
```

time: 164 us -> 52 us (0.32); the launches traced: 162 us -> 51.9 us
  blocking collectives: 65.1 us -> 0 us
  local copies, waits for them, and re-layouts: 47.5 us -> 1.7 us
  between operations: 13.6 us -> 0.19 us
  starting transfers between devices: 10.6 us -> 24 us
  Pallas kernels: 0 us -> 11.8 us
  matrix products: 11.6 us -> 0 us
  waiting for transfers between devices: 5.57 us -> 14.1 us
  other arithmetic: 8 us -> 0.12 us
    psum x2 -> x0, blocking collectives: 65.1 us -> none  [normalize(): lax.psum((jnp.sum(grouped, axis=(1, 3)), jnp.sum(grouped * grouped, axis=...]
    concatenate x10 -> x0, local copies, waits for them, and re-layouts: 20.4 us -> none  [tap_stack(): return jnp.concatenate(pieces, axis=-1).reshape(-1, 9 * width)]
    ppermute x8 -> x16, starting transfers between devices: 10.5 us -> 24 us  [the longest x12 20.4 us: shifted(): lax.ppermute(value, axis, [(i, (i + by) % size) for i in range(size)])]
    pallas_call x0 -> x7, Pallas kernels: none -> 11.8 us  [the longest x2 10.9 us: convolve(): pl.pallas_call(functools.partial(conv_body, pieces=len(pieces), others=le...]
    dot_general x2 -> x0, matrix products: 11.6 us -> none  [finish(): lax.dot_general(stacked, flat_kernel, (((1,), (1,)), ((), ())), preferred...]
    ppermute x8 -> x16, waiting for transfers between devices: 4.84 us -> 14.1 us  [the longest x2 10.1 us: gathered(): got = lax.ppermute(send, 'dp', [(0, 1), (1, 0)])]
    all_gather x2 -> x0, local copies, waits for them, and re-layouts: 8.4 us -> none  [convolve_gathered(): whole_kernel = lax.all_gather(kernel, 'dp', axis=0, tiled=True)]
    unnamed x27 -> x11, local copies, waits for them, and re-layouts: 9.62 us -> 1.35 us
  transfers between devices with their start and end apart: 10 -> 16, of which waited for: 3 -> 5; matrix products, arithmetic and copies ran while one was open for 24% -> 1% of each run, Pallas kernels for 0% -> 11%
where the time goes in v1:
time: 52 us; the launch traced here: 51.9 us
  starting transfers between devices  24 us (46%)
  waiting for transfers between devices  14.1 us (27%)
  Pallas kernels  11.8 us (23%)
  local copies, waits for them, and re-layouts  1.7 us (3%)
    ppermute x12, starting transfers between devices, shifted(): lax.ppermute(value, axis, [(i, (i + by) % size) for i in range(size)])  20.4 us
    pallas_call x2, Pallas kernels, convolve(): pl.pallas_call(functools.partial(conv_body, pieces=len(pieces), others=le...  10.9 us
    ppermute x2, waiting for transfers between devices, gathered(): got = lax.ppermute(send, 'dp', [(0, 1), (1, 0)])  10.1 us
    ppermute x12, waiting for transfers between devices, shifted(): lax.ppermute(value, axis, [(i, (i + by) % size) for i in range(size)])  4.03 us
    ppermute x2, starting transfers between devices, gathered(): got = lax.ppermute(send, 'dp', [(0, 1), (1, 0)])  3.63 us
    unnamed x11, local copies, waits for them, and re-layouts  1.35 us
  transfers between devices with their start and end apart: 16, of which 5 were waited for; matrix products, arithmetic and copies ran while one was open for 1% of the time, Pallas kernels for 11%

profile of v1, /device:TPU:0, one launch (start us, length us, event | category | flops | bytes accessed | tf_op | source)
XLA Modules:
  0.0 51.9 jit_solution(2800892981356476695)
XLA Ops:
  0.0 1.3 %copy-done.1 = bf16[160,9,320]{2,0,1:T(8,128)(2,1)S(1)} copy-done((bf16[160,9,320]{2,0,1:T(8,128)(2,1)S(1)}, bf16[160,9,320]{2,0,1:T(8,128)(2,1)}, u32[]{:S(2)}) %copy-start.1) | copy-done | bytes 921624
  1.3 0.3 pack.2
  1.6 3.0 %collective-permute-start.6 = (bf16[3,80,1024]{2,1,0:T(8,128)(2,1)S(1)}, bf16[3,80,1024]{2,1,0:T(8,128)(2,1)S(1)}, u32[]{:S(2)}, u32[]{:S(2)}) collective-permute-start(bf16[3,80,1024]{2,1,0:T(8,128)(2,1)S(1)} %get-tuple-element.29), channel_id=1, source_target_pairs={{0,16},{16,0},{1,17},{17,1},{2,18},{18,2},{3,19},{19,3},{4,20},{20... | collective-permute-start | bytes 1474568 | tf_op jit(solution)/shard_map/ppermute | solution.py:319
  4.6 0.3 first.1
  4.9 2.7 %collective-permute-start.2 = (bf16[16,320]{1,0:T(8,128)(2,1)S(1)}, bf16[16,320]{1,0:T(8,128)(2,1)S(1)}, u32[]{:S(2)}, u32[]{:S(2)}) collective-permute-start(bf16[16,320]{1,0:T(8,128)(2,1)S(1)} %get-tuple-element.24.refs_2_), channel_id=1, source_target_pairs={{0,8},{4,12},{8,0},{12,4},{1,9},{5,13},{9,1},{13,5},{2,10},{6,14},... | collective-permute-start | bytes 30728 | tf_op jit(solution)/shard_map/ppermute | solution.py:122
  7.6 1.6 %collective-permute-start = (bf16[48,320]{1,0:T(8,128)(2,1)S(1)}, bf16[48,320]{1,0:T(8,128)(2,1)S(1)}, u32[]{:S(2)}, u32[]{:S(2)}) collective-permute-start(bf16[48,320]{1,0:T(8,128)(2,1)S(1)} %get-tuple-element.22), channel_id=1, source_target_pairs={{0,4},{4,8},{8,12},{12,0},{1,5},{5,9},{9,13},{13,1},{2,6},{6,10},{... | collective-permute-start | bytes 92168 | tf_op jit(solution)/shard_map/ppermute | solution.py:122
  9.1 2.2 %collective-permute-start.1 = (bf16[48,320]{1,0:T(8,128)(2,1)S(1)}, bf16[48,320]{1,0:T(8,128)(2,1)S(1)}, u32[]{:S(2)}, u32[]{:S(2)}) collective-permute-start(bf16[48,320]{1,0:T(8,128)(2,1)S(1)} %get-tuple-element.23), channel_id=1, source_target_pairs={{0,12},{4,0},{8,4},{12,8},{1,13},{5,1},{9,5},{13,9},{2,14},{6,2},{... | collective-permute-start | bytes 92168 | tf_op jit(solution)/shard_map/ppermute | solution.py:122
  11.4 0.3 pack.3
  11.7 0.6 %collective-permute-start.14 = (bf16[3,80,1024]{2,1,0:T(8,128)(2,1)S(1)}, bf16[3,80,1024]{2,1,0:T(8,128)(2,1)S(1)}, u32[]{:S(2)}, u32[]{:S(2)}) collective-permute-start(bf16[3,80,1024]{2,1,0:T(8,128)(2,1)S(1)} %get-tuple-element.38), channel_id=1, source_target_pairs={{0,16},{16,0},{1,17},{17,1},{2,18},{18,2},{3,19},{19,3},{4,20},{20... | collective-permute-start | bytes 1474568 | tf_op jit(solution)/shard_map/ppermute | solution.py:319
  12.3 0.1 fusion.3
  12.3 4.4 %collective-permute-done.6.refs_10_ = bf16[3,80,1024]{2,1,0:T(8,128)(2,1)S(1)} collective-permute-done((bf16[3,80,1024]{2,1,0:T(8,128)(2,1)S(1)}, bf16[3,80,1024]{2,1,0:T(8,128)(2,1)S(1)}, u32[]{:S(2)}, u32[]{:S(2)}) %collective-permute-start.6) | collective-permute-done | bytes 491552 | tf_op jit(solution)/shard_map/ppermute | solution.py:319
  16.7 0.0 collective-permute-start.7
  16.7 0.0 collective-permute-done.2.refs_5_
  16.8 2.1 %collective-permute-start.5 = (bf16[16,320]{1,0:T(8,128)(2,1)S(1)}, bf16[16,320]{1,0:T(8,128)(2,1)S(1)}, u32[]{:S(2)}, u32[]{:S(2)}) collective-permute-start(bf16[16,320]{1,0:T(8,128)(2,1)S(1)} %get-tuple-element.25.refs_5_), channel_id=1, source_target_pairs={{0,2},{1,3},{2,0},{3,1},{4,6},{5,7},{6,4},{7,5},{8,10},{9,11},{10,... | collective-permute-start | bytes 30728 | tf_op jit(solution)/shard_map/ppermute | solution.py:122
  18.9 0.2 collective-permute-start.3
  19.2 1.5 %collective-permute-start.4 = (bf16[64,320]{1,0:T(8,128)(2,1)S(1)}, bf16[64,320]{1,0:T(8,128)(2,1)S(1)}, u32[]{:S(2)}, u32[]{:S(2)}) collective-permute-start(bf16[64,320]{1,0:T(8,128)(2,1)S(1)} %get-tuple-element.27), channel_id=1, source_target_pairs={{0,3},{1,0},{2,1},{3,2},{4,7},{5,4},{6,5},{7,6},{8,11},{9,8},{10,9... | collective-permute-start | bytes 122888 | tf_op jit(solution)/shard_map/ppermute | solution.py:122
  20.7 5.7 %collective-permute-done.14.refs_10_ = bf16[3,80,1024]{2,1,0:T(8,128)(2,1)S(1)} collective-permute-done((bf16[3,80,1024]{2,1,0:T(8,128)(2,1)S(1)}, bf16[3,80,1024]{2,1,0:T(8,128)(2,1)S(1)}, u32[]{:S(2)}, u32[]{:S(2)}) %collective-permute-start.14) | collective-permute-done | bytes 491552 | tf_op jit(solution)/shard_map/ppermute | solution.py:319
  26.4 0.0 collective-permute-start.15
  26.4 0.1 compare_convert_fusion.refs_4_
  26.6 5.0 %conv.1 = (bf16[32,32,320]{2,1,0:T(8,128)(2,1)S(1)}, bf16[48,320]{1,0:T(8,128)(2,1)S(1)}, bf16[48,320]{1,0:T(8,128)(2,1)S(1)}, bf16[16,320]{1,0:T(8,128)(2,1)S(1)}) custom-call(bf16[32,32,320]{2,1,0:T(8,128)(2,1)S(1)} %bitcast.14, bf16[48,320]{1,0:T(8,128)(2,1)S(1)} %collective-permute-done.refs_3_.refs_1_, ...), custom_call_target="tpu_custom_call" | custom-call | tf_op jit(solution)/shard_map/conv/pallas_call | solution.py:289
  31.6 0.0 copy-start.4
  31.6 2.9 %collective-permute-start.10 = (bf16[16,320]{1,0:T(8,128)(2,1)S(1)}, bf16[16,320]{1,0:T(8,128)(2,1)S(1)}, u32[]{:S(2)}, u32[]{:S(2)}) collective-permute-start(bf16[16,320]{1,0:T(8,128)(2,1)S(1)} %get-tuple-element.33.refs_2_), channel_id=1, source_target_pairs={{0,8},{4,12},{8,0},{12,4},{1,9},{5,13},{9,1},{13,5},{2,10},{6,14},... | collective-permute-start | bytes 30728 | tf_op jit(solution)/shard_map/ppermute | solution.py:122
  34.5 1.6 %collective-permute-start.8 = (bf16[48,320]{1,0:T(8,128)(2,1)S(1)}, bf16[48,320]{1,0:T(8,128)(2,1)S(1)}, u32[]{:S(2)}, u32[]{:S(2)}) collective-permute-start(bf16[48,320]{1,0:T(8,128)(2,1)S(1)} %get-tuple-element.31), channel_id=1, source_target_pairs={{0,4},{4,8},{8,12},{12,0},{1,5},{5,9},{9,13},{13,1},{2,6},{6,10},{... | collective-permute-start | bytes 92168 | tf_op jit(solution)/shard_map/ppermute | solution.py:122
  36.1 2.2 %collective-permute-start.9 = (bf16[48,320]{1,0:T(8,128)(2,1)S(1)}, bf16[48,320]{1,0:T(8,128)(2,1)S(1)}, u32[]{:S(2)}, u32[]{:S(2)}) collective-permute-start(bf16[48,320]{1,0:T(8,128)(2,1)S(1)} %get-tuple-element.32), channel_id=1, source_target_pairs={{0,12},{4,0},{8,4},{12,8},{1,13},{5,1},{9,5},{13,9},{2,14},{6,2},{... | collective-permute-start | bytes 92168 | tf_op jit(solution)/shard_map/ppermute | solution.py:122
  38.3 0.3 copy.8
  38.6 1.8 %collective-permute-done.8.refs_3_.refs_1_ = bf16[48,320]{1,0:T(8,128)(2,1)S(1)} collective-permute-done((bf16[48,320]{1,0:T(8,128)(2,1)S(1)}, bf16[48,320]{1,0:T(8,128)(2,1)S(1)}, u32[]{:S(2)}, u32[]{:S(2)}) %collective-permute-start.8) | collective-permute-done | bytes 30752 | tf_op jit(solution)/shard_map/ppermute | solution.py:122
  40.4 0.1 collective-permute-done.9.refs_4_.refs_2_
  40.5 0.1 collective-permute-start.11
  40.5 1.7 %collective-permute-start.12 = (bf16[64,320]{1,0:T(8,128)(2,1)S(1)}, bf16[64,320]{1,0:T(8,128)(2,1)S(1)}, u32[]{:S(2)}, u32[]{:S(2)}) collective-permute-start(bf16[64,320]{1,0:T(8,128)(2,1)S(1)} %get-tuple-element.36), channel_id=1, source_target_pairs={{0,3},{1,0},{2,1},{3,2},{4,7},{5,4},{6,5},{7,6},{8,11},{9,8},{10,9... | collective-permute-start | bytes 122888 | tf_op jit(solution)/shard_map/ppermute | solution.py:122
  42.3 1.5 %collective-permute-start.13 = (bf16[16,320]{1,0:T(8,128)(2,1)S(1)}, bf16[16,320]{1,0:T(8,128)(2,1)S(1)}, u32[]{:S(2)}, u32[]{:S(2)}) collective-permute-start(bf16[16,320]{1,0:T(8,128)(2,1)S(1)} %get-tuple-element.34.refs_5_), channel_id=1, source_target_pairs={{0,2},{1,3},{2,0},{3,1},{4,6},{5,7},{6,4},{7,5},{8,10},{9,11},{10,... | collective-permute-start | bytes 30728 | tf_op jit(solution)/shard_map/ppermute | solution.py:122
  43.8 2.2 %collective-permute-done.13.refs_8_ = bf16[16,320]{1,0:T(8,128)(2,1)S(1)} collective-permute-done((bf16[16,320]{1,0:T(8,128)(2,1)S(1)}, bf16[16,320]{1,0:T(8,128)(2,1)S(1)}, u32[]{:S(2)}, u32[]{:S(2)}) %collective-permute-start.13) | collective-permute-done | bytes 10272 | tf_op jit(solution)/shard_map/ppermute | solution.py:122
  46.0 5.9 %conv_skip.1 = bf16[32,32,320]{2,1,0:T(8,128)(2,1)} custom-call(bf16[32,32,320]{2,1,0:T(8,128)(2,1)S(1)} %get-tuple-element.30.refs_0_, bf16[48,320]{1,0:T(8,128)(2,1)S(1)} %collective-permute-done.8.refs_3_.refs_1_, bf16[48,320]{1,0:T(8,128)(2,1)S(1)} %collective-permute-done.9.refs_4_.refs_2_, f32[1,320]{1,0:T(1,128)S(1)} %broadcast_in_dim.12.refs_3_, ...), custom_call_target="tpu_custom_call" | custom-call | tf_op jit(solution)/shard_map/conv_skip/pallas_call | solution.py:289
  (25 shorter events, 0.1 us)
Async XLA Ops:
  0.0 4.6 %copy-start = (bf16[1,32,32,320]{3,2,1,0:T(8,128)(2,1)S(1)}, bf16[1,32,32,320]{3,2,1,0:T(8,128)(2,1)}, u32[]{:S(2)}) copy-start(bf16[1,32,32,320]{3,2,1,0:T(8,128)(2,1)} %param.5) | copy-start | bytes 1966084
  0.0 1.3 %copy-start.1 = (bf16[160,9,320]{2,0,1:T(8,128)(2,1)S(1)}, bf16[160,9,320]{2,0,1:T(8,128)(2,1)}, u32[]{:S(2)}) copy-start(bf16[160,9,320]{2,0,1:T(8,128)(2,1)} %param.7) | copy-start | bytes 2764804
  1.3 10.1 %copy-start.2 = (bf16[160,9,320]{2,0,1:T(8,128)(2,1)S(1)}, bf16[160,9,320]{2,0,1:T(8,128)(2,1)}, u32[]{:S(2)}) copy-start(bf16[160,9,320]{2,0,1:T(8,128)(2,1)} %param.9) | copy-start | bytes 2764804
  1.6 15.1 %collective-permute-start.6 = (bf16[3,80,1024]{2,1,0:T(8,128)(2,1)S(1)}, bf16[3,80,1024]{2,1,0:T(8,128)(2,1)S(1)}, u32[]{:S(2)}, u32[]{:S(2)}) collective-permute-start(bf16[3,80,1024]{2,1,0:T(8,128)(2,1)S(1)} %get-tuple-element.29), channel_id=1, source_target_pairs={{0,16},{16,0},{1,17},{17,1},{2,18},{18,2},{3,19},{19,3},{4,20},{20... | collective-permute-start | bytes 1474568 | tf_op jit(solution)/shard_map/ppermute | solution.py:319
  4.9 21.6 %copy-start.3 = (f32[320]{0:T(512)S(1)}, f32[320]{0:T(512)}, u32[]{:S(2)}) copy-start(f32[320]{0:T(512)} %param.6) | copy-start | bytes 3844
  4.9 11.8 %collective-permute-start.2 = (bf16[16,320]{1,0:T(8,128)(2,1)S(1)}, bf16[16,320]{1,0:T(8,128)(2,1)S(1)}, u32[]{:S(2)}, u32[]{:S(2)}) collective-permute-start(bf16[16,320]{1,0:T(8,128)(2,1)S(1)} %get-tuple-element.24.refs_2_), channel_id=1, source_target_pairs={{0,8},{4,12},{8,0},{12,4},{1,9},{5,13},{9,1},{13,5},{2,10},{6,14},... | collective-permute-start | bytes 30728 | tf_op jit(solution)/shard_map/ppermute | solution.py:122
  7.6 9.2 %collective-permute-start = (bf16[48,320]{1,0:T(8,128)(2,1)S(1)}, bf16[48,320]{1,0:T(8,128)(2,1)S(1)}, u32[]{:S(2)}, u32[]{:S(2)}) collective-permute-start(bf16[48,320]{1,0:T(8,128)(2,1)S(1)} %get-tuple-element.22), channel_id=1, source_target_pairs={{0,4},{4,8},{8,12},{12,0},{1,5},{5,9},{9,13},{13,1},{2,6},{6,10},{... | collective-permute-start | bytes 92168 | tf_op jit(solution)/shard_map/ppermute | solution.py:122
  9.1 7.6 %collective-permute-start.1 = (bf16[48,320]{1,0:T(8,128)(2,1)S(1)}, bf16[48,320]{1,0:T(8,128)(2,1)S(1)}, u32[]{:S(2)}, u32[]{:S(2)}) collective-permute-start(bf16[48,320]{1,0:T(8,128)(2,1)S(1)} %get-tuple-element.23), channel_id=1, source_target_pairs={{0,12},{4,0},{8,4},{12,8},{1,13},{5,1},{9,5},{13,9},{2,14},{6,2},{... | collective-permute-start | bytes 92168 | tf_op jit(solution)/shard_map/ppermute | solution.py:122
  11.7 14.7 %collective-permute-start.14 = (bf16[3,80,1024]{2,1,0:T(8,128)(2,1)S(1)}, bf16[3,80,1024]{2,1,0:T(8,128)(2,1)S(1)}, u32[]{:S(2)}, u32[]{:S(2)}) collective-permute-start(bf16[3,80,1024]{2,1,0:T(8,128)(2,1)S(1)} %get-tuple-element.38), channel_id=1, source_target_pairs={{0,16},{16,0},{1,17},{17,1},{2,18},{18,2},{3,19},{19,3},{4,20},{20... | collective-permute-start | bytes 1474568 | tf_op jit(solution)/shard_map/ppermute | solution.py:319
  16.7 9.9 %collective-permute-start.7 = (bf16[3,80,1024]{2,1,0:T(8,128)(2,1)S(1)}, bf16[3,80,1024]{2,1,0:T(8,128)(2,1)S(1)}, u32[]{:S(2)}, u32[]{:S(2)}) collective-permute-start(bf16[3,80,1024]{2,1,0:T(8,128)(2,1)S(1)} %collective-permute-done.6.refs_10_), channel_id=1, source_target_pairs={{0,1},{1,0},{2,3},{3,2},{4,5},{5,4},{6,7},{7,6},{8,9},{9,8},{10,11... | collective-permute-start | bytes 1474568 | tf_op jit(solution)/shard_map/ppermute | solution.py:320
  16.8 9.7 %collective-permute-start.5 = (bf16[16,320]{1,0:T(8,128)(2,1)S(1)}, bf16[16,320]{1,0:T(8,128)(2,1)S(1)}, u32[]{:S(2)}, u32[]{:S(2)}) collective-permute-start(bf16[16,320]{1,0:T(8,128)(2,1)S(1)} %get-tuple-element.25.refs_5_), channel_id=1, source_target_pairs={{0,2},{1,3},{2,0},{3,1},{4,6},{5,7},{6,4},{7,5},{8,10},{9,11},{10,... | collective-permute-start | bytes 30728 | tf_op jit(solution)/shard_map/ppermute | solution.py:122
  18.9 7.6 %collective-permute-start.3 = (bf16[64,320]{1,0:T(8,128)(2,1)S(1)}, bf16[64,320]{1,0:T(8,128)(2,1)S(1)}, u32[]{:S(2)}, u32[]{:S(2)}) collective-permute-start(bf16[64,320]{1,0:T(8,128)(2,1)S(1)} %get-tuple-element.26), channel_id=1, source_target_pairs={{0,1},{1,2},{2,3},{3,0},{4,5},{5,6},{6,7},{7,4},{8,9},{9,10},{10,1... | collective-permute-start | bytes 122888 | tf_op jit(solution)/shard_map/ppermute | solution.py:122
  19.2 7.4 %collective-permute-start.4 = (bf16[64,320]{1,0:T(8,128)(2,1)S(1)}, bf16[64,320]{1,0:T(8,128)(2,1)S(1)}, u32[]{:S(2)}, u32[]{:S(2)}) collective-permute-start(bf16[64,320]{1,0:T(8,128)(2,1)S(1)} %get-tuple-element.27), channel_id=1, source_target_pairs={{0,3},{1,0},{2,1},{3,2},{4,7},{5,4},{6,5},{7,6},{8,11},{9,8},{10,9... | collective-permute-start | bytes 122888 | tf_op jit(solution)/shard_map/ppermute | solution.py:122
  26.4 17.4 %collective-permute-start.15 = (bf16[3,80,1024]{2,1,0:T(8,128)(2,1)S(1)}, bf16[3,80,1024]{2,1,0:T(8,128)(2,1)S(1)}, u32[]{:S(2)}, u32[]{:S(2)}) collective-permute-start(bf16[3,80,1024]{2,1,0:T(8,128)(2,1)S(1)} %collective-permute-done.14.refs_10_), channel_id=1, source_target_pairs={{0,1},{1,0},{2,3},{3,2},{4,5},{5,4},{6,7},{7,6},{8,9},{9,8},{10,11... | collective-permute-start | bytes 1474568 | tf_op jit(solution)/shard_map/ppermute | solution.py:320
  31.6 12.2 %copy-start.4 = (f32[320]{0:T(512)S(1)}, f32[320]{0:T(512)}, u32[]{:S(2)}) copy-start(f32[320]{0:T(512)} %param.8) | copy-start | bytes 3844
  31.6 7.0 %collective-permute-start.10 = (bf16[16,320]{1,0:T(8,128)(2,1)S(1)}, bf16[16,320]{1,0:T(8,128)(2,1)S(1)}, u32[]{:S(2)}, u32[]{:S(2)}) collective-permute-start(bf16[16,320]{1,0:T(8,128)(2,1)S(1)} %get-tuple-element.33.refs_2_), channel_id=1, source_target_pairs={{0,8},{4,12},{8,0},{12,4},{1,9},{5,13},{9,1},{13,5},{2,10},{6,14},... | collective-permute-start | bytes 30728 | tf_op jit(solution)/shard_map/ppermute | solution.py:122
  34.5 5.9 %collective-permute-start.8 = (bf16[48,320]{1,0:T(8,128)(2,1)S(1)}, bf16[48,320]{1,0:T(8,128)(2,1)S(1)}, u32[]{:S(2)}, u32[]{:S(2)}) collective-permute-start(bf16[48,320]{1,0:T(8,128)(2,1)S(1)} %get-tuple-element.31), channel_id=1, source_target_pairs={{0,4},{4,8},{8,12},{12,0},{1,5},{5,9},{9,13},{13,1},{2,6},{6,10},{... | collective-permute-start | bytes 92168 | tf_op jit(solution)/shard_map/ppermute | solution.py:122
  36.1 4.4 %collective-permute-start.9 = (bf16[48,320]{1,0:T(8,128)(2,1)S(1)}, bf16[48,320]{1,0:T(8,128)(2,1)S(1)}, u32[]{:S(2)}, u32[]{:S(2)}) collective-permute-start(bf16[48,320]{1,0:T(8,128)(2,1)S(1)} %get-tuple-element.32), channel_id=1, source_target_pairs={{0,12},{4,0},{8,4},{12,8},{1,13},{5,1},{9,5},{13,9},{2,14},{6,2},{... | collective-permute-start | bytes 92168 | tf_op jit(solution)/shard_map/ppermute | solution.py:122
  40.5 5.5 %collective-permute-start.11 = (bf16[64,320]{1,0:T(8,128)(2,1)S(1)}, bf16[64,320]{1,0:T(8,128)(2,1)S(1)}, u32[]{:S(2)}, u32[]{:S(2)}) collective-permute-start(bf16[64,320]{1,0:T(8,128)(2,1)S(1)} %get-tuple-element.35), channel_id=1, source_target_pairs={{0,1},{1,2},{2,3},{3,0},{4,5},{5,6},{6,7},{7,4},{8,9},{9,10},{10,1... | collective-permute-start | bytes 122888 | tf_op jit(solution)/shard_map/ppermute | solution.py:122
  40.5 5.5 %collective-permute-start.12 = (bf16[64,320]{1,0:T(8,128)(2,1)S(1)}, bf16[64,320]{1,0:T(8,128)(2,1)S(1)}, u32[]{:S(2)}, u32[]{:S(2)}) collective-permute-start(bf16[64,320]{1,0:T(8,128)(2,1)S(1)} %get-tuple-element.36), channel_id=1, source_target_pairs={{0,3},{1,0},{2,1},{3,2},{4,7},{5,4},{6,5},{7,6},{8,11},{9,8},{10,9... | collective-permute-start | bytes 122888 | tf_op jit(solution)/shard_map/ppermute | solution.py:122
  42.3 3.7 %collective-permute-start.13 = (bf16[16,320]{1,0:T(8,128)(2,1)S(1)}, bf16[16,320]{1,0:T(8,128)(2,1)S(1)}, u32[]{:S(2)}, u32[]{:S(2)}) collective-permute-start(bf16[16,320]{1,0:T(8,128)(2,1)S(1)} %get-tuple-element.34.refs_5_), channel_id=1, source_target_pairs={{0,2},{1,3},{2,0},{3,1},{4,6},{5,7},{6,4},{7,5},{8,10},{9,11},{10,... | collective-permute-start | bytes 30728 | tf_op jit(solution)/shard_map/ppermute | solution.py:122

commit v2 on v1

v2 whole, which is shorter than its diff:
```python
import functools

import jax
import jax.numpy as jnp
from jax import lax
from jax.experimental import pallas as pl
from jax.experimental.pallas import tpu as pltpu
from jax.sharding import PartitionSpec as P


GROUPS = 32
EPS = 1e-05
ROWS = 16
F32 = jnp.float32
BF16 = jnp.bfloat16
MIB = 1 << 20


def split_rows(total, square):
    width = total.shape[1]
    at = lax.broadcasted_iota(jnp.int32, (ROWS, width), 0)
    out = jnp.zeros((ROWS, width), F32)
    for base, value in ((0, total), (3, square)):
        for step in range(3):
            part = value.astype(BF16).astype(F32)
            out = jnp.where(at == base + step, part, out)
            value = value - part
    return out.astype(BF16)


def join_rows(rows):
    return rows[0:1] + rows[1:2] + rows[2:3], rows[3:4] + rows[4:5] + rows[5:6]


def padded(size, to):
    return -(-size // to) * to


def padded_lanes(width):
    return padded(3 * width, 128)


def put_taps(store, taps, width):
    main = width // 128 * 128
    tail = width - main
    for e, tap in enumerate(taps):
        if main:
            store(e * main, main, tap[..., :main])
    if tail:
        for e, tap in enumerate(taps):
            store(3 * main + e * tail, tail, tap[..., main:])


def pack_body(kernel_ref, own_ref, send_ref, *, axis, parts):
    _, outs, width = kernel_ref.shape
    lanes = own_ref.shape[2]
    if 3 * width < lanes:
        own_ref[:, :, 3 * width :] = jnp.zeros((3, outs, lanes - 3 * width), BF16)
    for a in range(3):
        def store(at, size, value, a=a):
            own_ref[a, :, at : at + size] = value

        put_taps(store, [kernel_ref[3 * a + e] for e in range(3)], width)
    piece = outs // parts
    at = pl.multiple_of(lax.rem(lax.axis_index(axis), parts) * piece, ROWS)
    send_ref[...] = own_ref[:, pl.ds(at, piece), :]


def pack(kernel, axis, parts):
    outs, _, width = kernel.shape
    lanes = padded_lanes(width)
    return pl.pallas_call(
        functools.partial(pack_body, axis=axis, parts=parts),
        out_shape=(
            jax.ShapeDtypeStruct((3, outs, lanes), BF16),
            jax.ShapeDtypeStruct((3, outs // parts, lanes), BF16),
        ),
        compiler_params=pltpu.CompilerParams(vmem_limit_bytes=8 * MIB),
        name="pack",
    )(jnp.transpose(kernel, (1, 0, 2)))


def tile_stats(rows):
    return jnp.sum(rows, axis=0, keepdims=True), jnp.sum(rows * rows, axis=0, keepdims=True)


def carries(size, k):
    return any(abs(i - (i ^ k)) == 1 for i in range(size))


def faces_next(axis, k):
    me = lax.axis_index(axis)
    return (me ^ k) == me + 1


def faces_last(axis, k):
    me = lax.axis_index(axis)
    return (me ^ k) == me - 1


def put_messages(out_ref, stats, message_refs):
    length, cells, _ = out_ref.shape
    for i, ref in enumerate(message_refs):
        if ref.shape[0] > ROWS:
            ref[:cells] = out_ref[jnp.where(faces_next("row", i + 1), length - 1, 0)]
            ref[cells:] = stats
        else:
            ref[...] = stats


def first_body(tile_ref, *message_refs):
    length, cells, width = tile_ref.shape
    total = jnp.zeros((1, width), F32)
    square = jnp.zeros((1, width), F32)
    step = 4
    for at in range(0, length, step):
        rows = tile_ref[at : at + step].reshape(step * cells, width).astype(F32)
        one, two = tile_stats(rows)
        total, square = total + one, square + two
    put_messages(tile_ref, split_rows(total, square), message_refs)


def message_shapes(cells, width, axis):
    size = lax.axis_size(axis)
    rows = [cells + ROWS if carries(size, k) else ROWS for k in range(1, size)]
    return tuple(jax.ShapeDtypeStruct((n, width), BF16) for n in rows + [ROWS] * (size == 1))


def first_messages(tile):
    _, cells, width = tile.shape
    return pl.pallas_call(
        first_body,
        out_shape=message_shapes(cells, width, "row"),
        compiler_params=pltpu.CompilerParams(vmem_limit_bytes=8 * MIB),
        name="first",
    )(tile)


def exchange(messages, axis):
    size = lax.axis_size(axis)
    if size == 1:
        return list(messages)
    return [
        lax.ppermute(value, axis, [(i, i ^ (k + 1)) for i in range(size)])
        for k, value in enumerate(messages)
    ]


def summed(own, refs, size):
    rows = own.astype(F32)
    for ref in refs if size > 1 else ():
        rows = rows + ref[ref.shape[0] - ROWS :].astype(F32)
    return join_rows(rows)


def halos(refs, axis):
    before = after = None
    for i, ref in enumerate(refs):
        if ref.shape[0] > ROWS:
            value = ref[: ref.shape[0] - ROWS].astype(F32)
            before = value if before is None else jnp.where(faces_last(axis, i + 1), value, before)
            after = value if after is None else jnp.where(faces_next(axis, i + 1), value, after)
    return before, after


def edge_body(edge_ref, own_ref, *refs, size):
    got = max(size - 1, 1)
    row_refs, out_refs = refs[:got], refs[got:]
    _, length, width = edge_ref.shape
    own = own_ref[own_ref.shape[0] - ROWS :]
    total, square = summed(own, row_refs, size)
    stats = split_rows(total, square)
    above, below = halos(row_refs, "row")
    if above is None:
        above = below = jnp.zeros((1, width), F32)
    cells = above.shape[0]
    for i, ref in enumerate(out_refs):
        if ref.shape[0] > ROWS:
            rows = ref.shape[0] - ROWS
            right = faces_next("col", i + 1)
            top = jnp.where(right, above[cells - 1 : cells], above[0:1])
            bottom = jnp.where(right, below[cells - 1 : cells], below[0:1])
            filler = jnp.zeros((rows - length - 2, width), F32)
            middle = edge_ref[jnp.where(right, 1, 0)].astype(F32)
            ref[:rows] = jnp.concatenate([top, middle, bottom, filler], axis=0).astype(BF16)
            ref[rows:] = stats
        else:
            ref[...] = stats


def edge_messages(tile, own, got):
    length, _, width = tile.shape
    rows = padded(length + 2, ROWS)
    return pl.pallas_call(
        functools.partial(edge_body, size=lax.axis_size("row")),
        out_shape=message_shapes(rows, width, "col"),
        compiler_params=pltpu.CompilerParams(vmem_limit_bytes=8 * MIB),
        name="edge",
    )(jnp.stack([tile[:, 0], tile[:, -1]]), own, *got)


def conv_body(*refs, pieces, got, sizes, count, skip, place):
    tile_ref, gain_ref, ones_ref, own_ref = refs[:4]
    row_refs, col_refs = refs[4 : 4 + got[0]], refs[4 + got[0] : 4 + got[0] + got[1]]
    at = 4 + got[0] + got[1]
    piece_refs = refs[at : at + pieces]
    at += pieces
    if skip:
        skip_ref = refs[at]
        at += 1
    out_ref, message_refs = refs[at], refs[at + 1 : -4]
    taps_ref, weight_ref, edge_ref, sems = refs[-4:]

    length, cells, width = tile_ref.shape
    lanes = taps_ref.shape[2]
    copies = []
    for i, (piece, start) in enumerate(zip(piece_refs, place())):
        copy = pltpu.make_async_copy(
            piece, weight_ref.at[:, pl.ds(start, piece.shape[1]), :], sems.at[i]
        )
        copy.start()
        copies.append(copy)

    own = own_ref[own_ref.shape[0] - ROWS :]
    total, square = summed(own, col_refs, sizes[1])
    grouped = jnp.dot(split_rows(total, square), ones_ref[...], preferred_element_type=F32)
    total, square = join_rows(grouped)
    average = total / count
    spread = jnp.maximum(square / count - average * average, 0.0)
    scale = lax.rsqrt(spread + EPS) * gain_ref[...] * 0.5

    def act(value):
        half = (value.astype(F32) - average) * scale
        return half + half * jnp.tanh(half)

    row, col = lax.axis_index("row"), lax.axis_index("col")
    above, below = halos(row_refs, "row")
    left, right = halos(col_refs, "col")
    rows = edge_ref.shape[1]
    at = lax.broadcasted_iota(jnp.int32, (rows, width), 0)
    low = jnp.where(row > 0, 0, 1)
    high = jnp.where(row < sizes[0] - 1, length + 2, length + 1)
    held = (at >= low) & (at < high)
    for side, (edge, inside) in enumerate(((left, col > 0), (right, col < sizes[1] - 1))):
        if edge is None:
            edge_ref[side] = jnp.zeros((rows, width), F32)
        else:
            edge_ref[side] = jnp.where(held & inside, act(edge), 0.0)
    if 3 * width < lanes:
        taps_ref[:, :, 3 * width :] = jnp.zeros((length + 2, cells, lanes - 3 * width), BF16)
    where = lax.broadcasted_iota(jnp.int32, (cells, width), 0)

    def put_row(i, centre):
        left = jnp.where(where == 0, edge_ref[0, pl.ds(i, 1), :], pltpu.roll(centre, 1, 0))
        right = jnp.where(where == cells - 1, edge_ref[1, pl.ds(i, 1), :], pltpu.roll(centre, cells - 1, 0))

        def store(at, size, value):
            taps_ref[i, :, at : at + size] = value

        put_taps(store, [left.astype(BF16), centre.astype(BF16), right.astype(BF16)], width)

    def one_row(i, carry):
        put_row(i + 1, act(tile_ref[i]))
        return carry

    lax.fori_loop(0, length, one_row, 0, unroll=4)

    for i, source, inside in ((0, above, row > 0), (length + 1, below, row < sizes[0] - 1)):
        if source is None:
            put_row(i, jnp.zeros((cells, width), F32))
        else:
            put_row(i, jnp.where(inside, act(source), 0.0))

    for copy in copies:
        copy.wait()

    outs = out_ref.shape[2]
    step = 8
    total = jnp.zeros((1, outs), F32)
    square = jnp.zeros((1, outs), F32)
    for start in range(0, length, step):
        result = None
        for a in range(3):
            part = lax.dot_general(
                taps_ref[start + a : start + a + step].reshape(step * cells, lanes),
                weight_ref[a],
                (((1,), (1,)), ((), ())),
                preferred_element_type=F32,
            )
            result = part if result is None else result + part
        if skip:
            result = result + skip_ref[start : start + step].reshape(step * cells, outs).astype(F32)
            out_ref[start : start + step] = result.astype(BF16).reshape(step, cells, outs)
        else:
            rounded = result.astype(BF16)
            out_ref[start : start + step] = rounded.reshape(step, cells, outs)
            one, two = tile_stats(rounded.astype(F32))
            total, square = total + one, square + two
    if not skip:
        put_messages(out_ref, split_rows(total, square), message_refs)


def convolve(tile, gain, ones, own, row_got, col_got, pieces, place, count, skip):
    length, cells, width = tile.shape
    lanes = padded_lanes(width)
    out = (jax.ShapeDtypeStruct((length, cells, width), BF16),)
    if skip is None:
        out = out + message_shapes(cells, width, "row")
    vmem = pl.BlockSpec(memory_space=pltpu.VMEM)
    anywhere = pl.BlockSpec(memory_space=pl.ANY)
    skips = [] if skip is None else [skip]
    return pl.pallas_call(
        functools.partial(
            conv_body,
            pieces=len(pieces),
            got=(len(row_got), len(col_got)),
            sizes=(lax.axis_size("row"), lax.axis_size("col")),
            count=count,
            skip=skip is not None,
            place=place,
        ),
        in_specs=[vmem] * (4 + len(row_got) + len(col_got)) + [anywhere] * len(pieces) + [vmem] * len(skips),
        out_specs=(vmem,) * len(out),
        out_shape=out,
        scratch_shapes=[
            pltpu.VMEM((length + 2, cells, lanes), BF16),
            pltpu.VMEM((3, width, lanes), BF16),
            pltpu.VMEM((2, padded(length + 2, ROWS), width), F32),
            pltpu.SemaphoreType.DMA((len(pieces),)),
        ],
        compiler_params=pltpu.CompilerParams(vmem_limit_bytes=24 * MIB),
        name="conv_skip" if skips else "conv",
    )(tile, gain, ones, own, *row_got, *col_got, *pieces, *skips)


def gathered(kernel):
    outs = kernel.shape[0]
    cols = lax.axis_size("col")
    own, send = pack(kernel, "col", 2)

    def over(value):
        return lax.ppermute(value, "dp", [(0, 1), (1, 0)])

    def pair(value):
        return lax.ppermute(value, "col", [(i, i ^ 1) for i in range(cols)])

    piece = outs // 2

    def place():
        dp, half = lax.axis_index("dp"), lax.rem(lax.axis_index("col"), 2)
        other = (1 - dp) * outs
        return [
            pl.multiple_of(dp * outs, ROWS),
            pl.multiple_of(other + half * piece, ROWS),
            pl.multiple_of(other + (1 - half) * piece, ROWS),
        ]

    return own, send, over, pair, place


def whole_kernel(kernel):
    return pack(lax.all_gather(kernel, "dp", axis=0, tiled=True), "col", 1)[0]


def local(features, norm1_gain, conv1_kernel, norm2_gain, conv2_kernel):
    _, length, cells, width = features.shape
    members = width // GROUPS
    count = length * cells * lax.axis_size("row") * lax.axis_size("col") * members
    tile = features[0]
    group = jnp.arange(width) // members
    ones = (group[:, None] == group[None, :]).astype(BF16)
    split = lax.axis_size("dp") == 2 and lax.axis_size("col") % 2 == 0 and conv1_kernel.shape[0] % (2 * ROWS) == 0

    if split:
        own1, send1, over, pair, place = gathered(conv1_kernel)
        own2, send2 = gathered(conv2_kernel)[:2]
        got1 = over(send1)
        pieces1 = [own1, got1, pair(got1)]
        got2 = over(send2)
        pieces2 = [own2, got2, pair(got2)]
    else:
        pieces1, pieces2 = [whole_kernel(conv1_kernel)], [whole_kernel(conv2_kernel)]
        place = lambda: [0]

    messages = first_messages(tile)
    row_got = exchange(messages, "row")
    messages = edge_messages(tile, messages[-1], row_got)
    col_got = exchange(messages, "col")
    middle, *again = convolve(
        tile, norm1_gain[None], ones, messages[-1], row_got, col_got, pieces1, place, count, None
    )
    row_got = exchange(again, "row")
    messages = edge_messages(middle, again[-1], row_got)
    col_got = exchange(messages, "col")
    (result,) = convolve(
        middle, norm2_gain[None], ones, messages[-1], row_got, col_got, pieces2, place, count, tile
    )
    return result[None]


def solution(mesh):
    return jax.shard_map(
        local,
        mesh=mesh,
        in_specs=(P("dp", "row", "col", None), P(), P("dp", None, None), P(), P("dp", None, None)),
        out_specs=P("dp", "row", "col", None),
        check_vma=False,
    )
```

time: 52 us -> 53.3 us (1.025)
  waiting for transfers between devices: 14.1 us -> 22.4 us
  starting transfers between devices: 24 us -> 16.9 us
    ppermute x16, waiting for transfers between devices: 14.1 us -> 22.4 us  [the longest x2 13.8 us: over(): return lax.ppermute(value, 'dp', [(0, 1), (1, 0)])]
    ppermute x16, starting transfers between devices: 24 us -> 16.9 us  [the longest x12 13.5 us: exchange(): lax.ppermute(value, axis, [(i, i ^ k + 1) for i in range(size)])]
where the time goes in v2:
time: 53.3 us; the launch traced here: 53.1 us
  waiting for transfers between devices  22.4 us (42%)
  starting transfers between devices  16.9 us (32%)
  Pallas kernels  11.7 us (22%)
  local copies, waits for them, and re-layouts  1.7 us (3%)
    ppermute x2, waiting for transfers between devices, over(): return lax.ppermute(value, 'dp', [(0, 1), (1, 0)])  13.8 us
    ppermute x12, starting transfers between devices, exchange(): lax.ppermute(value, axis, [(i, i ^ k + 1) for i in range(size)])  13.5 us
    pallas_call x2, Pallas kernels, convolve(): pl.pallas_call(functools.partial(conv_body, pieces=len(pieces), got=(len(...  10.8 us
    ppermute x12, waiting for transfers between devices, exchange(): lax.ppermute(value, axis, [(i, i ^ k + 1) for i in range(size)])  8.65 us
    ppermute x2, starting transfers between devices, over(): return lax.ppermute(value, 'dp', [(0, 1), (1, 0)])  3.41 us
    unnamed x11, local copies, waits for them, and re-layouts  1.35 us
  transfers between devices with their start and end apart: 16, of which 5 were waited for; matrix products, arithmetic and copies ran while one was open for 1% of the time, Pallas kernels for 11%

profile of v2, /device:TPU:0, one launch (start us, length us, event | category | flops | bytes accessed | tf_op | source)
XLA Modules:
  0.0 53.1 jit_solution(8904124218699360096)
XLA Ops:
  0.0 1.3 %copy-done.1 = bf16[160,9,320]{2,0,1:T(8,128)(2,1)S(1)} copy-done((bf16[160,9,320]{2,0,1:T(8,128)(2,1)S(1)}, bf16[160,9,320]{2,0,1:T(8,128)(2,1)}, u32[]{:S(2)}) %copy-start.1) | copy-done | bytes 921624
  1.3 0.3 pack.2
  1.6 3.0 %collective-permute-start.6 = (bf16[3,80,1024]{2,1,0:T(8,128)(2,1)S(1)}, bf16[3,80,1024]{2,1,0:T(8,128)(2,1)S(1)}, u32[]{:S(2)}, u32[]{:S(2)}) collective-permute-start(bf16[3,80,1024]{2,1,0:T(8,128)(2,1)S(1)} %get-tuple-element.29), channel_id=1, source_target_pairs={{0,16},{16,0},{1,17},{17,1},{2,18},{18,2},{3,19},{19,3},{4,20},{20... | collective-permute-start | bytes 1474568 | tf_op jit(solution)/shard_map/ppermute | solution.py:342
  4.6 0.3 first.1
  4.9 2.7 %collective-permute-start.1 = (bf16[16,320]{1,0:T(8,128)(2,1)S(1)}, bf16[16,320]{1,0:T(8,128)(2,1)S(1)}, u32[]{:S(2)}, u32[]{:S(2)}) collective-permute-start(bf16[16,320]{1,0:T(8,128)(2,1)S(1)} %get-tuple-element.24), channel_id=1, source_target_pairs={{0,8},{4,12},{8,0},{12,4},{1,9},{5,13},{9,1},{13,5},{2,10},{6,14},... | collective-permute-start | bytes 30728 | tf_op jit(solution)/shard_map/ppermute | solution.py:144
  7.6 1.6 %collective-permute-start = (bf16[48,320]{1,0:T(8,128)(2,1)S(1)}, bf16[48,320]{1,0:T(8,128)(2,1)S(1)}, u32[]{:S(2)}, u32[]{:S(2)}) collective-permute-start(bf16[48,320]{1,0:T(8,128)(2,1)S(1)} %get-tuple-element.23), channel_id=1, source_target_pairs={{0,4},{4,0},{8,12},{12,8},{1,5},{5,1},{9,13},{13,9},{2,6},{6,2},{1... | collective-permute-start | bytes 92168 | tf_op jit(solution)/shard_map/ppermute | solution.py:144
  9.1 0.2 collective-permute-start.2
  9.4 0.3 pack.3
  9.6 0.4 collective-permute-start.14
  10.0 0.1 fusion.3
  10.1 6.6 %collective-permute-done.6.refs_11_ = bf16[3,80,1024]{2,1,0:T(8,128)(2,1)S(1)} collective-permute-done((bf16[3,80,1024]{2,1,0:T(8,128)(2,1)S(1)}, bf16[3,80,1024]{2,1,0:T(8,128)(2,1)S(1)}, u32[]{:S(2)}, u32[]{:S(2)}) %collective-permute-start.6) | collective-permute-done | bytes 491552 | tf_op jit(solution)/shard_map/ppermute | solution.py:342
  16.8 0.0 collective-permute-done.1.refs_1_.refs_5_
  16.8 0.0 collective-permute-done.refs_0_.refs_4_
  16.8 2.1 %collective-permute-start.4 = (bf16[16,320]{1,0:T(8,128)(2,1)S(1)}, bf16[16,320]{1,0:T(8,128)(2,1)S(1)}, u32[]{:S(2)}, u32[]{:S(2)}) collective-permute-start(bf16[16,320]{1,0:T(8,128)(2,1)S(1)} %get-tuple-element.27), channel_id=1, source_target_pairs={{0,2},{1,3},{2,0},{3,1},{4,6},{5,7},{6,4},{7,5},{8,10},{9,11},{10,... | collective-permute-start | bytes 30728 | tf_op jit(solution)/shard_map/ppermute | solution.py:144
  19.0 0.2 collective-permute-start.3
  19.2 0.0 collective-permute-start.5
  19.2 7.2 %collective-permute-done.14.refs_11_ = bf16[3,80,1024]{2,1,0:T(8,128)(2,1)S(1)} collective-permute-done((bf16[3,80,1024]{2,1,0:T(8,128)(2,1)S(1)}, bf16[3,80,1024]{2,1,0:T(8,128)(2,1)S(1)}, u32[]{:S(2)}, u32[]{:S(2)}) %collective-permute-start.14) | collective-permute-done | bytes 491552 | tf_op jit(solution)/shard_map/ppermute | solution.py:342
  26.4 0.1 compare_convert_fusion.refs_2_
  26.5 0.0 collective-permute-done.3.refs_7_
  26.6 0.0 collective-permute-done.5.refs_9_
  26.6 5.0 %conv.1 = (bf16[32,32,320]{2,1,0:T(8,128)(2,1)S(1)}, bf16[48,320]{1,0:T(8,128)(2,1)S(1)}, bf16[16,320]{1,0:T(8,128)(2,1)S(1)}, bf16[48,320]{1,0:T(8,128)(2,1)S(1)}) custom-call(bf16[32,32,320]{2,1,0:T(8,128)(2,1)S(1)} %bitcast.14, f32[1,320]{1,0:T(1,128)S(1)} %broadcast_in_dim.11.refs_1_, bf16[320,320]{1,0:T(8,128)(2,1)S(1)} %compare_convert_fusion.refs_2_, ...), custom_call_target="tpu_custom_call" | custom-call | tf_op jit(solution)/shard_map/conv/pallas_call | solution.py:312
  31.6 0.0 copy-start.4
  31.6 2.9 %collective-permute-start.9 = (bf16[16,320]{1,0:T(8,128)(2,1)S(1)}, bf16[16,320]{1,0:T(8,128)(2,1)S(1)}, u32[]{:S(2)}, u32[]{:S(2)}) collective-permute-start(bf16[16,320]{1,0:T(8,128)(2,1)S(1)} %get-tuple-element.33), channel_id=1, source_target_pairs={{0,8},{4,12},{8,0},{12,4},{1,9},{5,13},{9,1},{13,5},{2,10},{6,14},... | collective-permute-start | bytes 30728 | tf_op jit(solution)/shard_map/ppermute | solution.py:144
  34.5 1.6 %collective-permute-start.8 = (bf16[48,320]{1,0:T(8,128)(2,1)S(1)}, bf16[48,320]{1,0:T(8,128)(2,1)S(1)}, u32[]{:S(2)}, u32[]{:S(2)}) collective-permute-start(bf16[48,320]{1,0:T(8,128)(2,1)S(1)} %get-tuple-element.32), channel_id=1, source_target_pairs={{0,4},{4,0},{8,12},{12,8},{1,5},{5,1},{9,13},{13,9},{2,6},{6,2},{1... | collective-permute-start | bytes 92168 | tf_op jit(solution)/shard_map/ppermute | solution.py:144
  36.0 0.3 copy.11
  36.4 2.1 %collective-permute-done.8.refs_0_.refs_4_ = bf16[48,320]{1,0:T(8,128)(2,1)S(1)} collective-permute-done((bf16[48,320]{1,0:T(8,128)(2,1)S(1)}, bf16[48,320]{1,0:T(8,128)(2,1)S(1)}, u32[]{:S(2)}, u32[]{:S(2)}) %collective-permute-start.8) | collective-permute-done | bytes 30752 | tf_op jit(solution)/shard_map/ppermute | solution.py:144
  38.4 3.4 %collective-permute-done.10.refs_2_.refs_6_ = bf16[48,320]{1,0:T(8,128)(2,1)S(1)} collective-permute-done((bf16[48,320]{1,0:T(8,128)(2,1)S(1)}, bf16[48,320]{1,0:T(8,128)(2,1)S(1)}, u32[]{:S(2)}, u32[]{:S(2)}) %collective-permute-start.10) | collective-permute-done | bytes 30752 | tf_op jit(solution)/shard_map/ppermute | solution.py:144
  41.8 0.1 collective-permute-start.11
  41.9 1.6 %collective-permute-start.13 = (bf16[64,320]{1,0:T(8,128)(2,1)S(1)}, bf16[64,320]{1,0:T(8,128)(2,1)S(1)}, u32[]{:S(2)}, u32[]{:S(2)}) collective-permute-start(bf16[64,320]{1,0:T(8,128)(2,1)S(1)} %get-tuple-element.34.refs_3_), channel_id=1, source_target_pairs={{0,3},{1,2},{2,1},{3,0},{4,7},{5,6},{6,5},{7,4},{8,11},{9,10},{10,... | collective-permute-start | bytes 122888 | tf_op jit(solution)/shard_map/ppermute | solution.py:144
  43.5 0.5 collective-permute-start.12
  44.1 3.2 %collective-permute-done.12.refs_8_ = bf16[16,320]{1,0:T(8,128)(2,1)S(1)} collective-permute-done((bf16[16,320]{1,0:T(8,128)(2,1)S(1)}, bf16[16,320]{1,0:T(8,128)(2,1)S(1)}, u32[]{:S(2)}, u32[]{:S(2)}) %collective-permute-start.12) | collective-permute-done | bytes 10272 | tf_op jit(solution)/shard_map/ppermute | solution.py:144
  47.3 5.9 %conv_skip.1 = bf16[32,32,320]{2,1,0:T(8,128)(2,1)} custom-call(bf16[32,32,320]{2,1,0:T(8,128)(2,1)S(1)} %get-tuple-element.30.refs_0_, f32[1,320]{1,0:T(1,128)S(1)} %broadcast_in_dim.12.refs_1_, bf16[320,320]{1,0:T(8,128)(2,1)S(1)} %compare_convert_fusion.refs_2_, bf16[64,320]{1,0:T(8,128)(2,1)S(1)} %get-tuple-element.34.refs_3_, ...), custom_call_target="tpu_custom_call" | custom-call | tf_op jit(solution)/shard_map/conv_skip/pallas_call | solution.py:312
  (27 shorter events, 0.2 us)
Async XLA Ops:
  0.0 4.6 %copy-start = (bf16[1,32,32,320]{3,2,1,0:T(8,128)(2,1)S(1)}, bf16[1,32,32,320]{3,2,1,0:T(8,128)(2,1)}, u32[]{:S(2)}) copy-start(bf16[1,32,32,320]{3,2,1,0:T(8,128)(2,1)} %param.5) | copy-start | bytes 1966084
  0.0 1.3 %copy-start.1 = (bf16[160,9,320]{2,0,1:T(8,128)(2,1)S(1)}, bf16[160,9,320]{2,0,1:T(8,128)(2,1)}, u32[]{:S(2)}) copy-start(bf16[160,9,320]{2,0,1:T(8,128)(2,1)} %param.7) | copy-start | bytes 2764804
  1.3 8.0 %copy-start.2 = (bf16[160,9,320]{2,0,1:T(8,128)(2,1)S(1)}, bf16[160,9,320]{2,0,1:T(8,128)(2,1)}, u32[]{:S(2)}) copy-start(bf16[160,9,320]{2,0,1:T(8,128)(2,1)} %param.9) | copy-start | bytes 2764804
  1.6 15.1 %collective-permute-start.6 = (bf16[3,80,1024]{2,1,0:T(8,128)(2,1)S(1)}, bf16[3,80,1024]{2,1,0:T(8,128)(2,1)S(1)}, u32[]{:S(2)}, u32[]{:S(2)}) collective-permute-start(bf16[3,80,1024]{2,1,0:T(8,128)(2,1)S(1)} %get-tuple-element.29), channel_id=1, source_target_pairs={{0,16},{16,0},{1,17},{17,1},{2,18},{18,2},{3,19},{19,3},{4,20},{20... | collective-permute-start | bytes 1474568 | tf_op jit(solution)/shard_map/ppermute | solution.py:342
  4.9 21.6 %copy-start.3 = (f32[320]{0:T(512)S(1)}, f32[320]{0:T(512)}, u32[]{:S(2)}) copy-start(f32[320]{0:T(512)} %param.6) | copy-start | bytes 3844
  4.9 11.9 %collective-permute-start.1 = (bf16[16,320]{1,0:T(8,128)(2,1)S(1)}, bf16[16,320]{1,0:T(8,128)(2,1)S(1)}, u32[]{:S(2)}, u32[]{:S(2)}) collective-permute-start(bf16[16,320]{1,0:T(8,128)(2,1)S(1)} %get-tuple-element.24), channel_id=1, source_target_pairs={{0,8},{4,12},{8,0},{12,4},{1,9},{5,13},{9,1},{13,5},{2,10},{6,14},... | collective-permute-start | bytes 30728 | tf_op jit(solution)/shard_map/ppermute | solution.py:144
  7.6 9.2 %collective-permute-start = (bf16[48,320]{1,0:T(8,128)(2,1)S(1)}, bf16[48,320]{1,0:T(8,128)(2,1)S(1)}, u32[]{:S(2)}, u32[]{:S(2)}) collective-permute-start(bf16[48,320]{1,0:T(8,128)(2,1)S(1)} %get-tuple-element.23), channel_id=1, source_target_pairs={{0,4},{4,0},{8,12},{12,8},{1,5},{5,1},{9,13},{13,9},{2,6},{6,2},{1... | collective-permute-start | bytes 92168 | tf_op jit(solution)/shard_map/ppermute | solution.py:144
  9.1 7.7 %collective-permute-start.2 = (bf16[48,320]{1,0:T(8,128)(2,1)S(1)}, bf16[48,320]{1,0:T(8,128)(2,1)S(1)}, u32[]{:S(2)}, u32[]{:S(2)}) collective-permute-start(bf16[48,320]{1,0:T(8,128)(2,1)S(1)} %get-tuple-element.22.own_ref), channel_id=1, source_target_pairs={{0,12},{4,8},{8,4},{12,0},{1,13},{5,9},{9,5},{13,1},{2,14},{6,10},... | collective-permute-start | bytes 92168 | tf_op jit(solution)/shard_map/ppermute | solution.py:144
  9.6 16.8 %collective-permute-start.14 = (bf16[3,80,1024]{2,1,0:T(8,128)(2,1)S(1)}, bf16[3,80,1024]{2,1,0:T(8,128)(2,1)S(1)}, u32[]{:S(2)}, u32[]{:S(2)}) collective-permute-start(bf16[3,80,1024]{2,1,0:T(8,128)(2,1)S(1)} %get-tuple-element.38), channel_id=1, source_target_pairs={{0,16},{16,0},{1,17},{17,1},{2,18},{18,2},{3,19},{19,3},{4,20},{20... | collective-permute-start | bytes 1474568 | tf_op jit(solution)/shard_map/ppermute | solution.py:342
  16.7 9.9 %collective-permute-start.7 = (bf16[3,80,1024]{2,1,0:T(8,128)(2,1)S(1)}, bf16[3,80,1024]{2,1,0:T(8,128)(2,1)S(1)}, u32[]{:S(2)}, u32[]{:S(2)}) collective-permute-start(bf16[3,80,1024]{2,1,0:T(8,128)(2,1)S(1)} %collective-permute-done.6.refs_11_), channel_id=1, source_target_pairs={{0,1},{1,0},{2,3},{3,2},{4,5},{5,4},{6,7},{7,6},{8,9},{9,8},{10,11... | collective-permute-start | bytes 1474568 | tf_op jit(solution)/shard_map/ppermute | solution.py:345
  16.8 9.7 %collective-permute-start.4 = (bf16[16,320]{1,0:T(8,128)(2,1)S(1)}, bf16[16,320]{1,0:T(8,128)(2,1)S(1)}, u32[]{:S(2)}, u32[]{:S(2)}) collective-permute-start(bf16[16,320]{1,0:T(8,128)(2,1)S(1)} %get-tuple-element.27), channel_id=1, source_target_pairs={{0,2},{1,3},{2,0},{3,1},{4,6},{5,7},{6,4},{7,5},{8,10},{9,11},{10,... | collective-permute-start | bytes 30728 | tf_op jit(solution)/shard_map/ppermute | solution.py:144
  19.0 7.6 %collective-permute-start.3 = (bf16[64,320]{1,0:T(8,128)(2,1)S(1)}, bf16[64,320]{1,0:T(8,128)(2,1)S(1)}, u32[]{:S(2)}, u32[]{:S(2)}) collective-permute-start(bf16[64,320]{1,0:T(8,128)(2,1)S(1)} %get-tuple-element.26), channel_id=1, source_target_pairs={{0,1},{1,0},{2,3},{3,2},{4,5},{5,4},{6,7},{7,6},{8,9},{9,8},{10,11... | collective-permute-start | bytes 122888 | tf_op jit(solution)/shard_map/ppermute | solution.py:144
  19.2 7.4 %collective-permute-start.5 = (bf16[64,320]{1,0:T(8,128)(2,1)S(1)}, bf16[64,320]{1,0:T(8,128)(2,1)S(1)}, u32[]{:S(2)}, u32[]{:S(2)}) collective-permute-start(bf16[64,320]{1,0:T(8,128)(2,1)S(1)} %get-tuple-element.25.refs_3_), channel_id=1, source_target_pairs={{0,3},{1,2},{2,1},{3,0},{4,7},{5,6},{6,5},{7,4},{8,11},{9,10},{10,... | collective-permute-start | bytes 122888 | tf_op jit(solution)/shard_map/ppermute | solution.py:144
  26.4 17.7 %collective-permute-start.15 = (bf16[3,80,1024]{2,1,0:T(8,128)(2,1)S(1)}, bf16[3,80,1024]{2,1,0:T(8,128)(2,1)S(1)}, u32[]{:S(2)}, u32[]{:S(2)}) collective-permute-start(bf16[3,80,1024]{2,1,0:T(8,128)(2,1)S(1)} %collective-permute-done.14.refs_11_), channel_id=1, source_target_pairs={{0,1},{1,0},{2,3},{3,2},{4,5},{5,4},{6,7},{7,6},{8,9},{9,8},{10,11... | collective-permute-start | bytes 1474568 | tf_op jit(solution)/shard_map/ppermute | solution.py:345
  31.6 12.5 %copy-start.4 = (f32[320]{0:T(512)S(1)}, f32[320]{0:T(512)}, u32[]{:S(2)}) copy-start(f32[320]{0:T(512)} %param.8) | copy-start | bytes 3844
  31.6 4.8 %collective-permute-start.9 = (bf16[16,320]{1,0:T(8,128)(2,1)S(1)}, bf16[16,320]{1,0:T(8,128)(2,1)S(1)}, u32[]{:S(2)}, u32[]{:S(2)}) collective-permute-start(bf16[16,320]{1,0:T(8,128)(2,1)S(1)} %get-tuple-element.33), channel_id=1, source_target_pairs={{0,8},{4,12},{8,0},{12,4},{1,9},{5,13},{9,1},{13,5},{2,10},{6,14},... | collective-permute-start | bytes 30728 | tf_op jit(solution)/shard_map/ppermute | solution.py:144
  34.5 4.0 %collective-permute-start.8 = (bf16[48,320]{1,0:T(8,128)(2,1)S(1)}, bf16[48,320]{1,0:T(8,128)(2,1)S(1)}, u32[]{:S(2)}, u32[]{:S(2)}) collective-permute-start(bf16[48,320]{1,0:T(8,128)(2,1)S(1)} %get-tuple-element.32), channel_id=1, source_target_pairs={{0,4},{4,0},{8,12},{12,8},{1,5},{5,1},{9,13},{13,9},{2,6},{6,2},{1... | collective-permute-start | bytes 92168 | tf_op jit(solution)/shard_map/ppermute | solution.py:144
  36.0 5.8 %collective-permute-start.10 = (bf16[48,320]{1,0:T(8,128)(2,1)S(1)}, bf16[48,320]{1,0:T(8,128)(2,1)S(1)}, u32[]{:S(2)}, u32[]{:S(2)}) collective-permute-start(bf16[48,320]{1,0:T(8,128)(2,1)S(1)} %get-tuple-element.31.own_ref), channel_id=1, source_target_pairs={{0,12},{4,8},{8,4},{12,0},{1,13},{5,9},{9,5},{13,1},{2,14},{6,10},... | collective-permute-start | bytes 92168 | tf_op jit(solution)/shard_map/ppermute | solution.py:144
  41.8 5.4 %collective-permute-start.11 = (bf16[64,320]{1,0:T(8,128)(2,1)S(1)}, bf16[64,320]{1,0:T(8,128)(2,1)S(1)}, u32[]{:S(2)}, u32[]{:S(2)}) collective-permute-start(bf16[64,320]{1,0:T(8,128)(2,1)S(1)} %get-tuple-element.35), channel_id=1, source_target_pairs={{0,1},{1,0},{2,3},{3,2},{4,5},{5,4},{6,7},{7,6},{8,9},{9,8},{10,11... | collective-permute-start | bytes 122888 | tf_op jit(solution)/shard_map/ppermute | solution.py:144
  41.9 5.3 %collective-permute-start.13 = (bf16[64,320]{1,0:T(8,128)(2,1)S(1)}, bf16[64,320]{1,0:T(8,128)(2,1)S(1)}, u32[]{:S(2)}, u32[]{:S(2)}) collective-permute-start(bf16[64,320]{1,0:T(8,128)(2,1)S(1)} %get-tuple-element.34.refs_3_), channel_id=1, source_target_pairs={{0,3},{1,2},{2,1},{3,0},{4,7},{5,6},{6,5},{7,4},{8,11},{9,10},{10,... | collective-permute-start | bytes 122888 | tf_op jit(solution)/shard_map/ppermute | solution.py:144
  43.5 3.7 %collective-permute-start.12 = (bf16[16,320]{1,0:T(8,128)(2,1)S(1)}, bf16[16,320]{1,0:T(8,128)(2,1)S(1)}, u32[]{:S(2)}, u32[]{:S(2)}) collective-permute-start(bf16[16,320]{1,0:T(8,128)(2,1)S(1)} %get-tuple-element.36), channel_id=1, source_target_pairs={{0,2},{1,3},{2,0},{3,1},{4,6},{5,7},{6,4},{7,5},{8,10},{9,11},{10,... | collective-permute-start | bytes 30728 | tf_op jit(solution)/shard_map/ppermute | solution.py:144
